TPU v7x, 512 devices: a whole 4x8x8 slice. The times are simulated.
512 devices in a mesh: tp: 64 (over y, z_hi, core), ep: 8 (over x, z_lo).
Axes of the slice: x: 4, y: 8, z: 8 (z_hi: 4, z_lo: 2; z = z_hi * 2 + z_lo), core: 2. Of those that a mesh axis runs over, the one named last changes fastest.
Arguments:
- residual: bfloat16 [8, 7168, 256], P('ep', 'tp')
- out_grad: bfloat16 [8, 7168, 256], P('ep', 'tp'), may hold values from -6 to 6
- norm_gain: float32 [7168], P('tp'), may hold values from 0.25 to 1.75
- context: bfloat16 [8, 16384, 256], P('ep', 'tp'), may hold values from -0.3125 to 0.3125
- w_out: bfloat16 [7168, 16384], P('ep', 'tp'), may hold values from -0.046875 to 0.046875
- w_gate: bfloat16 [8, 7168, 2048], P('ep', 'tp'), may hold values from -0.0625 to 0.0625
- w_up: bfloat16 [8, 7168, 2048], P('ep', 'tp'), may hold values from -0.0625 to 0.0625
- w_down: bfloat16 [8, 7168, 2048], P('ep', 'tp'), may hold values from -0.125 to 0.125
- slot_token: int32 [8, 8, 8], P('ep'), may hold values from 0 to 255, as said below
- slot_count: int32 [8, 8], P('ep'), may hold values from 1 to 8, as said below
- slot_gate: float32 [8, 8, 8], P('ep'), may hold values from 0.25 to 2.5
Outputs:
- resid_grad: bfloat16 [8, 7168, 256], P('ep', 'tp')
- context_grad: bfloat16 [8, 16384, 256], P('ep', 'tp')
- w_out_grad: bfloat16 [7168, 16384], P('ep', 'tp')
- gate_grad: bfloat16 [8, 7168, 2048], P('ep', 'tp')
- up_grad: bfloat16 [8, 7168, 2048], P('ep', 'tp')
- down_grad: bfloat16 [8, 7168, 2048], P('ep', 'tp')
Inputs may be any that keep to these rules, and one draw needn't show every extreme that they name: `slot_token`: within one group and expert the 8 token positions are distinct; slots at or beyond slot_count are unused. `slot_count`: in every draw one expert has 8 tokens from every group.
All inputs are finite; a program needn't handle non-finite values.
Results may differ from a plain program's by a relative error of at most 0.014.
Values may be sent and summed in bfloat16 or wider, within the bound.
A program may use at most 64 MiB of HBM per device.

v0:
```python
import jax
import jax.numpy as jnp
from jax import lax
from jax.sharding import PartitionSpec as P

norm_eps = 1e-06


def contract_rows(left, right):
    return lax.dot_general(
        left, right, (((0,), (0,)), ((), ())), preferred_element_type=jnp.float32
    )


def contract_cols(left, right):
    return lax.dot_general(
        left, right, (((1,), (1,)), ((), ())), preferred_element_type=jnp.float32
    )


def activate(pre_gate, pre_up, hid_grad):
    sigmoid_gate = jax.nn.sigmoid(pre_gate)
    silu_gate = pre_gate * sigmoid_gate
    hidden = (silu_gate * pre_up).astype(jnp.bfloat16)
    d_gate = (hid_grad * pre_up * sigmoid_gate * (1.0 + pre_gate * (1.0 - sigmoid_gate))).astype(
        jnp.bfloat16
    )
    d_up = (hid_grad * silu_gate).astype(jnp.bfloat16)
    return (hidden, d_gate, d_up)


def shards(
    residual,
    out_grad,
    norm_gain,
    context,
    w_out,
    w_gate,
    w_up,
    w_down,
    slot_token,
    slot_count,
    slot_gate,
):
    tp_count = lax.axis_size("tp")
    stream = residual[0].astype(jnp.float32)
    grad_in = out_grad[0].astype(jnp.float32)
    feat_share, group_rows = stream.shape
    features = feat_share * tp_count
    square = lax.psum(jnp.sum(stream * stream, axis=0), "tp")
    inv_rms = lax.rsqrt(square / features + norm_eps)[None, :]
    normed = stream * inv_rms
    gain_col = norm_gain[:, None]
    inputs = (normed * gain_col).astype(jnp.bfloat16)
    slot_table = slot_token[0]
    capacity = slot_table.shape[1]
    live_mask = jnp.arange(capacity)[None, :] < slot_count[0][:, None]
    one_hot = (
        (slot_table[:, :, None] == jnp.arange(group_rows)[None, None, :]) & live_mask[:, :, None]
    ).astype(jnp.bfloat16)
    send_x = jnp.einsum("dt,ect->edc", inputs, one_hot, preferred_element_type=jnp.float32).astype(
        jnp.bfloat16
    )
    go_rows = jnp.einsum("dt,ect->edc", out_grad[0], one_hot, preferred_element_type=jnp.float32)
    send_go = (slot_gate[0][:, None, :] * go_rows).astype(jnp.bfloat16)
    recv_x, recv_go = (
        lax.all_to_all(send_x, "ep", split_axis=0, concat_axis=2, tiled=True),
        lax.all_to_all(send_go, "ep", split_axis=0, concat_axis=2, tiled=True),
    )
    rows_x = recv_x[0]
    rows_go = recv_go[0]
    gate_w = w_gate[0]
    up_w = w_up[0]
    down_w = w_down[0]
    gate_part = contract_rows(rows_x, gate_w)
    up_part = contract_rows(rows_x, up_w)
    hid_part = contract_rows(rows_go, down_w)
    pre_gate, pre_up, hid_grad = lax.psum((gate_part, up_part, hid_part), "tp")
    hidden, d_gate, d_up = activate(pre_gate, pre_up, hid_grad)
    down_grad = jnp.dot(rows_go, hidden, preferred_element_type=jnp.float32).astype(jnp.bfloat16)[
        None
    ]
    gate_grad = jnp.dot(rows_x, d_gate, preferred_element_type=jnp.float32).astype(jnp.bfloat16)[
        None
    ]
    up_grad = jnp.dot(rows_x, d_up, preferred_element_type=jnp.float32).astype(jnp.bfloat16)[None]
    slot_back = (contract_cols(gate_w, d_gate) + contract_cols(up_w, d_up)).astype(jnp.bfloat16)
    returned = lax.all_to_all(slot_back[None], "ep", split_axis=2, concat_axis=0, tiled=True)
    in_grad = jnp.einsum(
        "edc,ect->dt", returned, one_hot, preferred_element_type=jnp.float32
    ).astype(jnp.bfloat16)
    scaled = in_grad.astype(jnp.float32) * gain_col
    dots = lax.psum(jnp.sum(scaled * normed, axis=0), "tp")
    resid = (grad_in + inv_rms * (scaled - normed * (dots / features)[None, :])).astype(
        jnp.bfloat16
    )
    full_grad = lax.all_gather(resid, "tp", axis=0, tiled=True)
    grad_block = lax.all_to_all(full_grad, "ep", split_axis=0, concat_axis=1, tiled=True)
    ctx_local = context[0]
    ctx_all = lax.all_gather(ctx_local, "ep", axis=1, tiled=True)
    weight_sum = contract_cols(grad_block, ctx_all)
    ctx_total = contract_rows(lax.all_gather(w_out, "ep", axis=0, tiled=True), full_grad)
    return (
        resid[None],
        ctx_total.astype(jnp.bfloat16)[None],
        weight_sum.astype(jnp.bfloat16),
        gate_grad,
        up_grad,
        down_grad,
    )


def solution(mesh):
    return jax.shard_map(
        shards,
        mesh=mesh,
        in_specs=(
            P("ep", "tp", None),
            P("ep", "tp", None),
            P("tp"),
            P("ep", "tp", None),
            P("ep", "tp"),
            P("ep", "tp", None),
            P("ep", "tp", None),
            P("ep", "tp", None),
            P("ep", None, None),
            P("ep", None),
            P("ep", None, None),
        ),
        out_specs=(
            P("ep", "tp", None),
            P("ep", "tp", None),
            P("ep", "tp"),
            P("ep", "tp", None),
            P("ep", "tp", None),
            P("ep", "tp", None),
        ),
        check_vma=False,
    )
```

profile of v0, /device:TPU:1, one launch (start us, length us, event | category | flops | bytes accessed | tf_op | source)
XLA Modules:
  0.0 1148.3 jit_solution(9309882180991946875)
XLA Ops:
  7.2 0.9 fusion.32
  8.1 145.8 %psum.35 = f32[256]{0:T(256)S(1)} all-reduce(f32[256]{0:T(256)S(1)} %fusion.32), channel_id=1, replica_groups=mesh['tp'=64,'ep'=8] {'tp'}, use_global_device_ids=true, to_apply=%region_1.0 | all-reduce | flops 256 | bytes 2048 | tf_op jit(solution)/shard_map/psum | solution.py:50
  153.9 0.7 iota_compare_fusion.1
  154.6 1.6 fusion.9
  156.3 4.9 all-to-all-start.1
  161.2 1.6 fusion.11
  162.9 3.4 all-to-all-done.1
  166.3 3.3 all-to-all-start
  169.7 1.0 fusion.16
  170.7 2.1 fusion.19
  172.8 1.8 all-to-all-done
  174.6 2.0 fusion.21
  176.7 560.9 %all-reduce.3.cloned.1.call-done = (f32[64,2048]{1,0:T(8,128)}, f32[64,2048]{1,0:T(8,128)}, f32[64,2048]{1,0:T(8,128)}) async-done(((f32[64,2048]{1,0:T(8,128)}, f32[64,2048]{1,0:T(8,128)}, f32[64,2048]{1,0:T(8,128)}), (f32[64,2048]{1,0:T(8,128)}, f32[64,2048]{1,0:T(8,128)}, f32[64,2048]{1,0:T(8,128)})) %all-reduce.3.cloned.1.call-update) | async-done | bytes 1572880 | tf_op jit(solution)/shard_map/psum | solution.py:78
  737.6 1.6 multiply_convert_fusion.1
  739.9 0.5 broadcast.36
  740.4 0.7 reduce
  741.2 9.0 all_to_all.67
  750.7 140.6 %psum.39 = f32[256]{0:T(256)S(1)} all-reduce(f32[256]{0:T(256)S(1)} %get-tuple-element.35), channel_id=1, replica_groups=mesh['tp'=64,'ep'=8] {'tp'}, use_global_device_ids=true, to_apply=%region_6.0 | all-reduce | flops 256 | bytes 2048 | tf_op jit(solution)/shard_map/psum | solution.py:93
  891.2 0.7 fusion.31
  892.0 0.7 all-gather.7.cloned.1.call-update
  892.6 82.2 %all-gather.5.cloned.1.call-done = bf16[7168,256]{1,0:T(8,128)(2,1)} async-done(((bf16[112,256]{1,0:T(8,128)(2,1)}), bf16[7168,256]{1,0:T(8,128)(2,1)}) %all-gather.5.cloned.1.call-update) | async-done | bytes 3670032 | tf_op jit(solution)/shard_map/all_gather | solution.py:97
  974.8 6.2 copy.32
  981.0 5.7 all-to-all-start.3
  986.8 0.5 all-gather.9.cloned.1.call-update
  987.3 1.1 fusion
  988.4 1.1 fusion.1
  989.5 1.1 fusion.2
  990.6 108.7 %all-gather.7.cloned.1.call-done = bf16[7168,256]{1,0:T(8,128)(2,1)} async-done(((bf16[896,256]{1,0:T(8,128)(2,1)}), bf16[7168,256]{1,0:T(8,128)(2,1)}) %all-gather.7.cloned.1.call-update) | async-done | bytes 3670032 | tf_op jit(solution)/shard_map/all_gather | solution.py:102
  1099.2 4.3 fusion.3
  1103.6 0.8 copy.33
  1104.3 33.2 %all-gather.9.cloned.1.call-done = bf16[1,256,2048]{2,1,0:T(8,128)(2,1)} async-done(((bf16[1,256,256]{2,1,0:T(8,128)(2,1)}), bf16[1,256,2048]{2,1,0:T(8,128)(2,1)}) %all-gather.9.cloned.1.call-update) | async-done | bytes 1048592 | tf_op jit(solution)/shard_map/all_gather | solution.py:100
  1137.5 4.3 convolution_convert_fusion.3
  (31 shorter events, 1.3 us)
Async XLA Ops:
  7.2 162.5 %copy-start = (bf16[1,112,2048]{2,1,0:T(8,128)(2,1)S(1)}, bf16[1,112,2048]{2,1,0:T(8,128)(2,1)}, u32[]{:S(2)}) copy-start(bf16[1,112,2048]{2,1,0:T(8,128)(2,1)} %param.16) | copy-start | bytes 1376260
  156.3 10.0 all-to-all-start.1
  166.3 8.3 all-to-all-start
  169.6 569.9 %copy-start.1 = (bf16[1,112,2048]{2,1,0:T(8,128)(2,1)S(1)}, bf16[1,112,2048]{2,1,0:T(8,128)(2,1)}, u32[]{:S(2)}) copy-start(bf16[1,112,2048]{2,1,0:T(8,128)(2,1)} %param.17) | copy-start | bytes 1376260
  169.6 568.0 %all-reduce.3.cloned.1.call-start = ((), (), s32[]{:S(2)}) async-start(), calls=%async_computation.7 | async-start | bytes 3145728 | tf_op jit(solution)/shard_map/psum | solution.py:78
  170.7 579.6 %copy-start.4 = (bf16[1,112,256]{2,1,0:T(8,128)(2,1)S(1)}, bf16[1,112,256]{2,1,0:T(8,128)(2,1)}, u32[]{:S(2)}) copy-start(bf16[1,112,256]{2,1,0:T(8,128)(2,1)} %param.11) | copy-start | bytes 172036
  170.7 579.6 %copy-start.6 = (s32[1,8,8]{2,1,0:T(8,128)S(1)}, s32[1,8,8]{2,1,0:T(8,128)}, u32[]{:S(2)}) copy-start(s32[1,8,8]{2,1,0:T(8,128)} %param.19) | copy-start | bytes 772
  170.7 579.7 %copy-start.7 = (f32[112]{0:T(128)S(1)}, f32[112]{0:T(128)}, u32[]{:S(2)}) copy-start(f32[112]{0:T(128)} %param.13) | copy-start | bytes 1348
  170.7 720.5 %copy-start.5 = (bf16[1,112,256]{2,1,0:T(8,128)(2,1)S(1)}, bf16[1,112,256]{2,1,0:T(8,128)(2,1)}, u32[]{:S(2)}) copy-start(bf16[1,112,256]{2,1,0:T(8,128)(2,1)} %param.12) | copy-start | bytes 172036
  176.7 798.1 %all-gather.5.cloned.1.call-start = ((), (), s32[]{:S(2)}) async-start(), calls=%async_computation.4 | async-start | bytes 3727360 | tf_op jit(solution)/shard_map/all_gather | solution.py:97
  891.9 207.3 %all-gather.7.cloned.1.call-start = ((), (), s32[]{:S(2)}) async-start(), calls=%async_computation.5 | async-start | bytes 4128768 | tf_op jit(solution)/shard_map/all_gather | solution.py:102
  981.0 8.4 copy-start.2
  981.0 8.4 copy-start.3
  981.0 156.4 %all-to-all-start.3 = ((bf16[8,896,256]{1,2,0:T(8,128)(2,1)}), bf16[8,896,256]{1,2,0:T(8,128)(2,1)}, u32[]{:S(2)}, u32[]{:S(2)}) async-start(bf16[8,896,256]{1,2,0:T(8,128)(2,1)} %copy.32), calls=%async_computation.3 | async-start | bytes 7340032 | tf_op jit(solution)/shard_map/all_to_all | solution.py:98
  986.7 150.7 %all-gather.9.cloned.1.call-start = ((), (), s32[]{:S(2)}) async-start(), calls=%async_computation.6 | async-start | bytes 1179648 | tf_op jit(solution)/shard_map/all_gather | solution.py:100
Sparse Core Ops, SparseCore 0:
  176.8 560.7 all-reduce.2
  892.0 82.7 all-gather.4
  977.1 122.0 all-gather.6
  1101.3 36.1 all-gather.8
where the time goes:
time: 1150 us
  waiting for transfers between devices  791 us (69%)
  blocking collectives  295 us (26%)
  matrix products  21.1 us (2%)
  starting transfers between devices  14.1 us (1%)
  between operations  13.9 us (1%)
    psum x1, waiting for transfers between devices, shards(): pre_gate, pre_up, hid_grad = lax.psum((gate_part, up_part, hid_part), 'tp')  561 us
    psum x1, blocking collectives, shards(): square = lax.psum(jnp.sum(stream * stream, axis=0), 'tp')  146 us
    psum x1, blocking collectives, shards(): dots = lax.psum(jnp.sum(scaled * normed, axis=0), 'tp')  141 us
    all_gather x1, waiting for transfers between devices, shards(): lax.all_gather(w_out, 'ep', axis=0, tiled=True)  109 us
    all_gather x1, waiting for transfers between devices, shards(): full_grad = lax.all_gather(resid, 'tp', axis=0, tiled=True)  82.2 us
    all_gather x1, waiting for transfers between devices, shards(): ctx_all = lax.all_gather(ctx_local, 'ep', axis=1, tiled=True)  33.2 us
  transfers between devices with their start and end apart: 7, of which 6 were waited for; matrix products, arithmetic and copies ran while one was open for 2% of the time, Pallas kernels for 0%

commit v1 on v0

v1 whole, which is shorter than its diff:
```python
import functools

import jax
import jax.numpy as jnp
from jax import lax
from jax.experimental import pallas as pl
from jax.experimental.pallas import tpu as pltpu
from jax.sharding import PartitionSpec as P

norm_eps = 1e-06
MESH = pl.DeviceIdType.MESH
BF = jnp.bfloat16
F32 = jnp.float32


def mm(left, right):
    return lax.dot_general(
        left, right, (((1,), (0,)), ((), ())), preferred_element_type=F32
    )


def mm_nt(left, right):
    return lax.dot_general(
        left, right, (((1,), (1,)), ((), ())), preferred_element_type=F32
    )


def mm_tn(left, right):
    return lax.dot_general(
        left, right, (((0,), (0,)), ((), ())), preferred_element_type=F32
    )


def eye_mask(n):
    rows = lax.broadcasted_iota(jnp.int32, (n, n), 0)
    cols = lax.broadcasted_iota(jnp.int32, (n, n), 1)
    return rows == cols


def col_to_row(col):
    n = col.shape[0]
    return jnp.sum(
        jnp.where(eye_mask(n), jnp.broadcast_to(col, (n, n)), 0.0), axis=0, keepdims=True
    )


def row_to_col(row):
    n = row.shape[1]
    return jnp.sum(
        jnp.where(eye_mask(n), jnp.broadcast_to(row, (n, n)), 0.0), axis=1, keepdims=True
    )


def kernel(
    dims,
    res_ref,
    og_ref,
    gain_ref,
    ctx_ref,
    wo_ref,
    wg_ref,
    wu_ref,
    wd_ref,
    tok_send_x,
    tok_send_go,
    send_scale,
    tok_slot,
    resid_out,
    ctx_out,
    wo_out,
    gate_out,
    up_out,
    down_out,
    a_send,
    a_recv,
    og_all,
    ctx_all,
    sel_all,
    sel_perm,
    part_out,
    part_own,
    core_recv,
    part1,
    y_recv,
    part2,
    z_recv,
    tile_sq,
    tile_sq_c,
    tile_sq_y,
    tile_sq_z,
    tile_dot,
    tile_dot_c,
    tile_dot_y,
    tile_dot_z,
    inv_buf,
    dot_buf,
    act,
    ret_send,
    ret_recv,
    delta_own,
    delta_all,
    base_send,
    base_recv,
    wo_acc,
    msg_send,
    msg_recv,
    sem_a,
    sem_ogt,
    sem_oga,
    sem_ogb,
    sem_ogk,
    sem_ctx,
    sem_sel,
    sem_core,
    sem_y,
    sem_z,
    sem_sqc,
    sem_sqy,
    sem_sqz,
    sem_dtc,
    sem_dty,
    sem_dtz,
    sem_actz,
    sem_acty,
    sem_actk,
    sem_ret,
    sem_dt,
    sem_da,
    sem_db,
    sem_dk,
    sem_base,
    sem_msg,
):
    NE, NY, NZ, CAP, FS, T, A, H, D = dims
    S = NE * CAP
    SZ = S // NZ
    HC = H // 2
    HY = HC // NY
    TH = T // 2
    SH = S // 2

    ep = lax.axis_index("ep")
    tp = lax.axis_index("tp")
    y = tp // (NZ * 2)
    c = tp % (NZ * 2)
    z = c // 2
    k = c % 2

    def tp_of(yy, zz, kk):
        return (yy * NZ + zz) * 2 + kk

    def ep_dev(i):
        return {"ep": (ep + i) % NE, "tp": tp}

    def y_dev(i):
        return {"ep": ep, "tp": tp_of((y + i) % NY, z, k)}

    def z_dev(i):
        return {"ep": ep, "tp": tp_of(y, (z + i) % NZ, k)}

    sib = {"ep": ep, "tp": tp_of(y, z, 1 - k)}
    cross = {"ep": y, "tp": tp_of(ep, z, k)}
    diag = ep == y

    def remote(src, dst, sems, i, dev):
        return pltpu.make_async_remote_copy(
            src_ref=src,
            dst_ref=dst,
            send_sem=sems.at[0, i],
            recv_sem=sems.at[1, i],
            device_id=dev,
            device_id_type=MESH,
        )

    started = []

    def go(copies):
        for one in copies:
            one.start()
        started.extend(copies)
        return copies

    def arrive(copies):
        for one in copies:
            one.wait_recv()

    barrier = pltpu.get_barrier_semaphore()
    for i in range(1, NE):
        pl.semaphore_signal(barrier, inc=1, device_id=ep_dev(i), device_id_type=MESH)
    for i in range(1, NY):
        pl.semaphore_signal(barrier, inc=1, device_id=y_dev(i), device_id_type=MESH)
    for i in range(1, NZ):
        pl.semaphore_signal(barrier, inc=1, device_id=z_dev(i), device_id_type=MESH)
    pl.semaphore_signal(barrier, inc=1, device_id=sib, device_id_type=MESH)

    @pl.when(jnp.logical_not(diag))
    def _():
        pl.semaphore_signal(barrier, inc=1, device_id=cross, device_id_type=MESH)

    def one_hot(tokens_ref, rows):
        lanes = lax.broadcasted_iota(jnp.int32, (rows, T), 1)
        return jnp.where(tokens_ref[...] == lanes, 1.0, 0.0).astype(BF)

    picked = mm_nt(one_hot(tok_send_x, 2 * S), res_ref[...]) + mm_nt(
        one_hot(tok_send_go, 2 * S), og_ref[...]
    )
    a_send[...] = (send_scale[...] * picked).astype(BF).reshape(NE, 2 * CAP, FS)

    peers = NE - 1 + NY - 1 + NZ
    pl.semaphore_wait(barrier, jnp.where(diag, peers, peers + 1))

    a_copies = go(
        [
            remote(a_send.at[(ep + i) % NE], a_recv.at[ep], sem_a, i, ep_dev(i))
            for i in range(1, NE)
        ]
    )
    og_cross = remote(og_ref, og_all.at[ep, z, k], sem_ogt, 0, cross)

    @pl.when(jnp.logical_not(diag))
    def _():
        og_cross.start()

    @pl.when(diag)
    def _():
        og_all[ep, z, k] = og_ref[...]

    a_recv[ep] = a_send[ep]
    ctx_copies = go(
        [remote(ctx_ref, ctx_all.at[ep], sem_ctx, i, ep_dev(i)) for i in range(1, NE)]
    )
    oh_slot = one_hot(tok_slot, S)
    sel_all[ep] = mm_nt(oh_slot, ctx_ref[...]).astype(BF)
    sel_copies = go(
        [remote(sel_all.at[ep], sel_all.at[ep], sem_sel, i, ep_dev(i)) for i in range(1, NE)]
    )
    ctx_all[ep] = ctx_ref[...]

    arrive(a_copies)
    rows = a_recv[...].astype(F32).reshape(NE, 2, CAP, FS)
    rows_x = rows[:, 0].reshape(S, FS)
    rows_go = rows[:, 1].reshape(S, FS)
    rows_xg = (rows_x * gain_ref[...]).astype(BF)
    rows_gob = rows_go.astype(BF)
    other = pl.ds(pl.multiple_of((1 - k) * HC, HC), HC)
    own = pl.ds(pl.multiple_of(k * HC, HC), HC)
    lefts = (rows_xg, rows_xg, rows_gob)
    weights = (wg_ref, wu_ref, wd_ref)
    for n in range(3):
        part_out[n] = mm(lefts[n], weights[n][:, other]).astype(BF)
    core_copies = go([remote(part_out, core_recv, sem_core, 0, sib)])
    sq_row = col_to_row(jnp.sum(rows_x * rows_x, axis=1, keepdims=True))
    tile_sq[0] = jnp.broadcast_to(sq_row, (8, S))
    sqc = go([remote(tile_sq.at[0], tile_sq_c, sem_sqc, 0, sib)])

    @pl.when(jnp.logical_not(diag))
    def _():
        og_cross.wait_recv()

    oga1 = go(
        [
            remote(
                og_all.at[y, z, k, :, pl.ds(0, TH)],
                og_all.at[y, z, k, :, pl.ds(0, TH)],
                sem_oga,
                i,
                y_dev(i),
            )
            for i in range(1, NY)
        ]
    )
    ogb1 = go(
        [
            remote(
                og_all.at[y, z, k, :, pl.ds(TH, TH)],
                og_all.at[y, z, k, :, pl.ds(TH, TH)],
                sem_ogb,
                i,
                z_dev(i),
            )
            for i in range(1, NZ)
        ]
    )

    for n in range(3):
        part_own[n] = mm(lefts[n], weights[n][:, own])

    arrive(core_copies)
    part1[...] = (part_own[...] + core_recv[...].astype(F32)).astype(BF)

    def y_cols(i):
        return pl.ds(pl.multiple_of(((y + i) % NY) * HY, HY), HY)

    y_copies = go(
        [
            remote(part1.at[:, :, y_cols(i)], y_recv.at[i - 1], sem_y, i, y_dev(i))
            for i in range(1, NY)
        ]
    )
    arrive(sqc)
    tile_sq[1] = tile_sq[0] + tile_sq_c[...]
    sqy = go(
        [remote(tile_sq.at[1], tile_sq_y.at[i - 1], sem_sqy, i, y_dev(i)) for i in range(1, NY)]
    )
    arrive(y_copies)
    total = part1[:, :, y_cols(0)].astype(F32)
    for i in range(1, NY):
        total = total + y_recv[i - 1].astype(F32)
    part2[...] = total.astype(BF)

    def z_rows(i):
        return pl.ds(pl.multiple_of(((z + i) % NZ) * SZ, SZ), SZ)

    z_copies = go(
        [
            remote(part2.at[:, z_rows(i), :], z_recv.at[i - 1], sem_z, i, z_dev(i))
            for i in range(1, NZ)
        ]
    )
    arrive(sqy)
    sq = tile_sq[1]
    for i in range(1, NY):
        sq = sq + tile_sq_y[i - 1]
    tile_sq[2] = sq
    sqz = go(
        [remote(tile_sq.at[2], tile_sq_z.at[i - 1], sem_sqz, i, z_dev(i)) for i in range(1, NZ)]
    )
    arrive(sqz)
    sq = tile_sq[2]
    for i in range(1, NZ):
        sq = sq + tile_sq_z[i - 1]
    inv_col = row_to_col(lax.rsqrt(sq[0:1] / D + norm_eps))
    inv_buf[...] = jnp.broadcast_to(inv_col, (S, 128))
    arrive(z_copies)
    total = part2[:, z_rows(0), :].astype(F32)
    for i in range(1, NZ):
        total = total + z_recv[i - 1].astype(F32)
    inv_mine = inv_buf[z_rows(0), 0:HY] if HY <= 128 else inv_buf[z_rows(0), 0:1]
    pre_gate = inv_mine * total[0]
    pre_up = inv_mine * total[1]
    hid_grad = total[2]
    sigmoid_gate = jax.nn.sigmoid(pre_gate)
    silu_gate = pre_gate * sigmoid_gate
    hidden = (silu_gate * pre_up).astype(BF)
    d_gate = (hid_grad * pre_up * sigmoid_gate * (1.0 + pre_gate * (1.0 - sigmoid_gate))).astype(BF)
    d_up = (hid_grad * silu_gate).astype(BF)
    my_cols = pl.ds(pl.multiple_of(k * HC + y * HY, HY), HY)
    act[0, z_rows(0), my_cols] = d_gate
    act[1, z_rows(0), my_cols] = d_up
    act[2, z_rows(0), my_cols] = hidden

    mine = act.at[:, z_rows(0), my_cols]
    actz = go([remote(mine, mine, sem_actz, i, z_dev(i)) for i in range(1, NZ)])
    dots = jnp.sum(d_gate.astype(F32) * pre_gate + d_up.astype(F32) * pre_up, axis=1, keepdims=True)
    dot_buf[...] = jnp.zeros_like(dot_buf)
    dot_buf[z_rows(0), :] = jnp.broadcast_to(dots, (SZ, 128))
    tile_dot[0] = jnp.broadcast_to(col_to_row(dot_buf[:, 0:1]), (8, S))
    dtz = go(
        [remote(tile_dot.at[0], tile_dot_z.at[i - 1], sem_dtz, i, z_dev(i)) for i in range(1, NZ)]
    )
    arrive(actz)
    mine_y = act.at[:, :, my_cols]
    acty = go([remote(mine_y, mine_y, sem_acty, i, y_dev(i)) for i in range(1, NY)])
    arrive(dtz)
    dt = tile_dot[0]
    for i in range(1, NZ):
        dt = dt + tile_dot_z[i - 1]
    tile_dot[1] = dt
    dty = go(
        [remote(tile_dot.at[1], tile_dot_y.at[i - 1], sem_dty, i, y_dev(i)) for i in range(1, NY)]
    )

    arrive(oga1)
    oga2 = go(
        [
            remote(
                og_all.at[:, z, k, :, pl.ds(0, TH)],
                og_all.at[:, z, k, :, pl.ds(0, TH)],
                sem_oga,
                NY + i,
                z_dev(i),
            )
            for i in range(1, NZ)
        ]
    )
    arrive(ogb1)
    ogb2 = go(
        [
            remote(
                og_all.at[y, :, k, :, pl.ds(TH, TH)],
                og_all.at[y, :, k, :, pl.ds(TH, TH)],
                sem_ogb,
                NZ + i,
                y_dev(i),
            )
            for i in range(1, NY)
        ]
    )

    arrive(acty)
    mine_k = act.at[:, :, own]
    actk = go([remote(mine_k, mine_k, sem_actk, 0, sib)])
    arrive(dty)
    dt = tile_dot[1]
    for i in range(1, NY):
        dt = dt + tile_dot_y[i - 1]
    tile_dot[2] = dt
    dtc = go([remote(tile_dot.at[2], tile_dot_c, sem_dtc, 0, sib)])
    arrive(dtc)
    dots_col = row_to_col((tile_dot[2] + tile_dot_c[...])[0:1])
    inv_col = inv_buf[:, 0:1]
    normed = rows_x * inv_col
    arrive(actk)
    slot_back = (
        (mm_nt(act[0], wg_ref[...]) + mm_nt(act[1], wu_ref[...])).astype(BF).astype(F32)
    )
    delta = inv_col * (gain_ref[...] * slot_back - normed * (dots_col / D))
    delta_own[...] = delta.astype(BF)

    d_cross = remote(delta_own, delta_all.at[z, k, ep], sem_dt, 0, cross)

    @pl.when(jnp.logical_not(diag))
    def _():
        d_cross.start()

    @pl.when(diag)
    def _():
        delta_all[z, k, ep] = delta_own[...]

    ret_send[...] = delta.reshape(NE, CAP, FS)
    ret_recv[ep] = ret_send[ep]
    ret_copies = go(
        [
            remote(ret_send.at[(ep + i) % NE], ret_recv.at[ep], sem_ret, i, ep_dev(i))
            for i in range(1, NE)
        ]
    )

    slot_in = (normed * gain_ref[...]).astype(BF)
    gate_out[...] = mm_tn(slot_in, act[0]).astype(BF)

    @pl.when(jnp.logical_not(diag))
    def _():
        d_cross.wait_recv()

    da = delta_all.at[z, k, y, pl.ds(0, SH)]
    db = delta_all.at[z, k, y, pl.ds(SH, SH)]
    da1 = go([remote(da, da, sem_da, i, y_dev(i)) for i in range(1, NY)])
    db1 = go([remote(db, db, sem_db, i, z_dev(i)) for i in range(1, NZ)])
    up_out[...] = mm_tn(slot_in, act[1]).astype(BF)
    down_out[...] = mm_tn(rows_gob, act[2]).astype(BF)
    arrive(db1)
    db = delta_all.at[:, k, y, pl.ds(SH, SH)]
    db2 = go([remote(db, db, sem_db, NZ + i, y_dev(i)) for i in range(1, NY)])
    arrive(da1)
    da = delta_all.at[z, k, :, pl.ds(0, SH)]
    da2 = go([remote(da, da, sem_da, NY + i, z_dev(i)) for i in range(1, NZ)])

    arrive(ogb2)
    arrive(oga2)
    ogk_mine = og_all.at[:, :, k]
    ogk = go([remote(ogk_mine, ogk_mine, sem_ogk, 0, sib)])
    arrive(sel_copies)
    sel = sel_all[...].astype(F32).reshape(NE, NE, CAP, A)
    for e in range(NE):
        sel_perm[e] = sel[:, e].reshape(S, A).astype(BF)
    arrive(ctx_copies)
    arrive(da2)
    arrive(db2)
    dk_mine = delta_all.at[:, k]
    dk = go([remote(dk_mine, dk_mine, sem_dk, 0, sib)])
    arrive(ogk)
    BL = NZ * 2 * FS
    for g in range(NE):
        block = og_all[g].reshape(BL, T)
        base_send[g] = mm_tn(wo_ref[...], block).astype(BF)
        one = mm_nt(block, ctx_all[g])
        if g == 0:
            wo_acc[...] = one
        else:
            wo_acc[...] += one
    base_recv[ep] = base_send[ep]
    base_copies = go(
        [
            remote(base_send.at[(ep + i) % NE], base_recv.at[ep], sem_base, i, ep_dev(i))
            for i in range(1, NE)
        ]
    )

    arrive(dk)
    slots = None
    for q in range(NZ * 2):
        feats = pl.ds(q * FS, FS)
        block = delta_all[q // 2, q % 2].reshape(NE * S, FS)
        one = mm(block, wo_ref[feats, :])
        slots = one if slots is None else slots + one
    slots = slots.reshape(NE, NE, CAP, A)
    for g in range(NE):
        msg_send[g] = slots[:, g].reshape(S, A).astype(BF)
    msg_recv[ep] = msg_send[ep]
    msg_copies = go(
        [
            remote(msg_send.at[(ep + i) % NE], msg_recv.at[ep], sem_msg, i, ep_dev(i))
            for i in range(1, NE)
        ]
    )
    right = sel_perm[...].reshape(NE * S, A)
    for q in range(NZ * 2):
        feats = pl.ds(q * FS, FS)
        block = delta_all[q // 2, q % 2].reshape(NE * S, FS)
        wo_out[feats, :] = (wo_acc[feats, :] + mm_tn(block, right)).astype(BF)

    arrive(ret_copies)
    returned = ret_recv[...].reshape(S, FS).astype(BF)
    resid_out[...] = (og_ref[...].astype(F32) + mm_tn(returned, oh_slot)).astype(BF)

    arrive(base_copies)
    total = base_recv[0].astype(F32)
    for i in range(1, NE):
        total = total + base_recv[i].astype(F32)
    arrive(msg_copies)
    picked = msg_recv[0].astype(F32)
    for i in range(1, NE):
        picked = picked + msg_recv[i].astype(F32)
    ctx_out[...] = (total + mm_tn(picked.astype(BF), oh_slot)).astype(BF)

    for one in started:
        one.wait_send()

    @pl.when(jnp.logical_not(diag))
    def _():
        og_cross.wait_send()
        d_cross.wait_send()


def shards(
    dims,
    residual,
    out_grad,
    norm_gain,
    context,
    w_out,
    w_gate,
    w_up,
    w_down,
    slot_token,
    slot_count,
    slot_gate,
):
    NE, NY, NZ, CAP, FS, T, A, H, D = dims
    S = NE * CAP
    BL = NZ * 2 * FS
    table = slot_token[0]
    live = jnp.arange(CAP)[None, :] < slot_count[0][:, None]
    table = jnp.where(live, table, -1)
    none = jnp.full_like(table, -1)
    tok_x = jnp.stack([table, none], axis=1).reshape(2 * S, 1)
    tok_go = jnp.stack([none, table], axis=1).reshape(2 * S, 1)
    scale = jnp.stack([jnp.ones_like(slot_gate[0]), slot_gate[0]], axis=1).reshape(2 * S, 1)
    tok_slot = table.reshape(S, 1)
    HC = H // 2
    HY = HC // NY
    SZ = S // NZ
    V = pltpu.VMEM
    dma = pltpu.SemaphoreType.DMA
    whole = pl.BlockSpec(memory_space=pltpu.VMEM)
    out_shape = (
        jax.ShapeDtypeStruct((FS, T), BF),
        jax.ShapeDtypeStruct((A, T), BF),
        jax.ShapeDtypeStruct((BL, A), BF),
        jax.ShapeDtypeStruct((FS, H), BF),
        jax.ShapeDtypeStruct((FS, H), BF),
        jax.ShapeDtypeStruct((FS, H), BF),
    )
    scratch = [
        V((NE, 2 * CAP, FS), BF),
        V((NE, 2 * CAP, FS), BF),
        V((NE, NZ, 2, FS, T), BF),
        V((NE, A, T), BF),
        V((NE, S, A), BF),
        V((NE, S, A), BF),
        V((3, S, HC), BF),
        V((3, S, HC), F32),
        V((3, S, HC), BF),
        V((3, S, HC), BF),
        V((NY - 1, 3, S, HY), BF),
        V((3, S, HY), BF),
        V((NZ - 1, 3, SZ, HY), BF),
        V((3, 8, S), F32),
        V((8, S), F32),
        V((NY - 1, 8, S), F32),
        V((NZ - 1, 8, S), F32),
        V((3, 8, S), F32),
        V((8, S), F32),
        V((NY - 1, 8, S), F32),
        V((NZ - 1, 8, S), F32),
        V((S, 128), F32),
        V((S, 128), F32),
        V((3, S, H), BF),
        V((NE, CAP, FS), F32),
        V((NE, CAP, FS), F32),
        V((S, FS), BF),
        V((NZ, 2, NE, S, FS), BF),
        V((NE, A, T), BF),
        V((NE, A, T), BF),
        V((BL, A), F32),
        V((NE, S, A), BF),
        V((NE, S, A), BF),
        dma((2, NE)),
        dma((2, 1)),
        dma((2, NY + NZ)),
        dma((2, NY + NZ)),
        dma((2, 1)),
        dma((2, NE)),
        dma((2, NE)),
        dma((2, 1)),
        dma((2, NY)),
        dma((2, NZ)),
        dma((2, 1)),
        dma((2, NY)),
        dma((2, NZ)),
        dma((2, 1)),
        dma((2, NY)),
        dma((2, NZ)),
        dma((2, NZ)),
        dma((2, NY)),
        dma((2, 1)),
        dma((2, NE)),
        dma((2, 1)),
        dma((2, NY + NZ)),
        dma((2, NY + NZ)),
        dma((2, 1)),
        dma((2, NE)),
        dma((2, NE)),
    ]
    resid, ctx_grad, wo_grad, gate_grad, up_grad, down_grad = pl.pallas_call(
        functools.partial(kernel, dims),
        out_shape=out_shape,
        in_specs=[whole] * 12,
        out_specs=[whole] * 6,
        scratch_shapes=scratch,
        compiler_params=pltpu.CompilerParams(
            collective_id=0, has_side_effects=True, vmem_limit_bytes=48 * 1024 * 1024
        ),
    )(
        residual[0],
        out_grad[0],
        norm_gain.reshape(1, FS),
        context[0],
        w_out,
        w_gate[0],
        w_up[0],
        w_down[0],
        tok_x,
        tok_go,
        scale,
        tok_slot,
    )
    return (
        resid[None],
        ctx_grad[None],
        wo_grad,
        gate_grad[None],
        up_grad[None],
        down_grad[None],
    )


def solution(mesh):
    sizes = dict(mesh.shape)
    NE = sizes["ep"]
    NY = NE
    NZ = sizes["tp"] // (2 * NY)

    def run(residual, out_grad, norm_gain, context, w_out, w_gate, w_up, w_down, *slots):
        D, T = residual.shape[1:]
        dims = (
            NE,
            NY,
            NZ,
            slots[0].shape[2],
            D // sizes["tp"],
            T,
            context.shape[1] // sizes["tp"],
            w_gate.shape[2],
            D,
        )
        return jax.shard_map(
            functools.partial(shards, dims),
            mesh=mesh,
            in_specs=(
                P("ep", "tp", None),
                P("ep", "tp", None),
                P("tp"),
                P("ep", "tp", None),
                P("ep", "tp"),
                P("ep", "tp", None),
                P("ep", "tp", None),
                P("ep", "tp", None),
                P("ep", None, None),
                P("ep", None),
                P("ep", None, None),
            ),
            out_specs=(
                P("ep", "tp", None),
                P("ep", "tp", None),
                P("ep", "tp"),
                P("ep", "tp", None),
                P("ep", "tp", None),
                P("ep", "tp", None),
            ),
            check_vma=False,
        )(residual, out_grad, norm_gain, context, w_out, w_gate, w_up, w_down, *slots)

    return run
```

time: 1150 us -> 127 us (0.11)
  waiting for transfers between devices: 791 us -> 0 us
  blocking collectives: 295 us -> 0 us
  Pallas kernels: 0 us -> 114 us
  matrix products: 21.1 us -> 0 us
  starting transfers between devices: 14.1 us -> 0 us
  between operations: 13.9 us -> 0.73 us
    psum x1 -> x0, waiting for transfers between devices: 561 us -> none  [shards(): pre_gate, pre_up, hid_grad = lax.psum((gate_part, up_part, hid_part), 'tp')]
    psum x2 -> x0, blocking collectives: 286 us -> none  [the longest x1 146 us: shards(): square = lax.psum(jnp.sum(stream * stream, axis=0), 'tp')]
    all_gather x3 -> x0, waiting for transfers between devices: 224 us -> none  [the longest x1 109 us: shards(): lax.all_gather(w_out, 'ep', axis=0, tiled=True)]
    pallas_call x0 -> x1, Pallas kernels: none -> 114 us  [shards(): pl.pallas_call(functools.partial(kernel, dims), out_shape=out_shape, in_s...]
    dot_general x13 -> x0, matrix products: 21.1 us -> none  [the longest x4 9.47 us: contract_rows(): lax.dot_general(left, right, (((0,), (0,)), ((), ())), preferred_element_...]
    all_to_all x3 -> x0, starting transfers between devices: 14 us -> none  [the longest x1 5.7 us: shards(): lax.all_to_all(full_grad, 'ep', split_axis=0, concat_axis=1, tiled=True)]
  transfers between devices with their start and end apart: 7 -> 0, of which waited for: 6 -> 0; matrix products, arithmetic and copies ran while one was open for 2% -> 0% of each run, Pallas kernels for 0% -> 0%
where the time goes in v1:
time: 127 us; the launch traced here: 126 us
  Pallas kernels  114 us (90%)
  local copies, waits for them, and re-layouts  10.8 us (9%)
    pallas_call x1, Pallas kernels, shards(): pl.pallas_call(functools.partial(kernel, dims), out_shape=out_shape, in_s...  114 us
    unnamed x28, local copies, waits for them, and re-layouts  10.3 us

profile of v1, /device:TPU:1, one launch (start us, length us, event | category | flops | bytes accessed | tf_op | source)
XLA Modules:
  0.0 125.6 jit_solution(14589210114579287296)
XLA Ops:
  0.6 0.0 copy-start.8
  0.6 0.0 copy-start.10
  0.7 0.7 copy-done.10
  1.3 0.1 iota_compare_fusion
  1.4 0.0 copy-done.8
  1.4 0.1 bitcast_select_fusion
  1.5 0.0 copy-start.9
  1.5 0.1 lt.46
  1.5 0.6 copy-done.9
  2.2 0.1 squeeze.31
  2.2 0.0 copy-start.4
  2.3 0.1 reshape.110.tok_send_go
  2.4 0.0 copy-start.5
  2.4 0.0 copy-start.6
  2.4 0.1 reshape.111.send_scale
  2.5 0.0 copy-start.7
  2.5 0.1 reshape.109.tok_send_x
  2.6 0.6 copy-done.4
  3.2 0.0 copy-done.5
  3.2 0.0 copy-done.6
  3.2 0.0 copy-done.7
  3.2 1.0 copy-done
  4.2 1.0 copy-done.1
  5.3 1.0 copy-done.2
  6.3 1.0 copy-done.3
  7.3 114.0 %shard_map.154 = (bf16[112,256]{1,0:T(8,128)(2,1)S(1)}, bf16[256,256]{1,0:T(8,128)(2,1)S(1)}, bf16[896,256]{1,0:T(8,128)(2,1)S(1)}, bf16[112,2048]{1,0:T(8,128)(...) custom-call(bf16[112,256]{1,0:T(8,128)(2,1)S(1)} %bitcast.29, bf16[112,256]{1,0:T(8,128)(2,1)S(1)} %bitcast.30, ...), custom_call_target="tpu_custom_call" | custom-call | tf_op jit(solution)/shard_map/pallas_call | solution.py:636
  121.3 0.6 copy.34
  121.9 0.7 copy.35
  122.6 0.8 copy.36
  123.3 0.8 copy.37
  124.1 0.8 copy.38
  124.9 0.8 copy.39
  (7 shorter events, 0.0 us)
Async XLA Ops:
  0.6 0.7 copy-start.8
  0.6 0.7 copy-start.10
  1.5 0.7 copy-start.9
  2.2 0.9 copy-start.4
  2.4 0.8 copy-start.5
  2.4 0.9 copy-start.6
  2.5 0.8 copy-start.7
  3.2 1.0 copy-start
  4.2 1.0 copy-start.1
  5.3 1.0 copy-start.2
  6.3 1.0 copy-start.3

commit v2 on v0

v2 whole, which is shorter than its diff:
```python
import functools

import jax
import jax.numpy as jnp
from jax import lax
from jax.experimental import pallas as pl
from jax.experimental.pallas import tpu as pltpu
from jax.sharding import PartitionSpec as P

norm_eps = 1e-06
MESH = pl.DeviceIdType.MESH
BF = jnp.bfloat16
F32 = jnp.float32


def mm(left, right):
    return lax.dot_general(
        left, right, (((1,), (0,)), ((), ())), preferred_element_type=F32
    )


def mm_nt(left, right):
    return lax.dot_general(
        left, right, (((1,), (1,)), ((), ())), preferred_element_type=F32
    )


def mm_tn(left, right):
    return lax.dot_general(
        left, right, (((0,), (0,)), ((), ())), preferred_element_type=F32
    )


def eye_mask(n):
    rows = lax.broadcasted_iota(jnp.int32, (n, n), 0)
    cols = lax.broadcasted_iota(jnp.int32, (n, n), 1)
    return rows == cols


def col_to_row(col):
    n = col.shape[0]
    return jnp.sum(
        jnp.where(eye_mask(n), jnp.broadcast_to(col, (n, n)), 0.0), axis=0, keepdims=True
    )


def row_to_col(row):
    n = row.shape[1]
    return jnp.sum(
        jnp.where(eye_mask(n), jnp.broadcast_to(row, (n, n)), 0.0), axis=1, keepdims=True
    )


def kernel(dims, spec, *refs):
    NE, NY, NZ, CAP, FS, T, A, H, D = dims
    NX = NE // 2
    S = NE * CAP
    SZ = S // NZ
    HC = H // 2
    HY = HC // NY
    TH = T // 2
    SH = S // 2
    RA = 32
    RB = FS - RA
    BL = NZ * 2 * FS
    R = Refs(spec, refs)

    ep = lax.axis_index("ep")
    tp = lax.axis_index("tp")
    y = tp // (NZ * 2)
    c = tp % (NZ * 2)
    z = c // 2
    k = c % 2
    x = ep // 2
    w = ep % 2

    def tp_of(yy, zz, kk):
        return (yy * NZ + zz) * 2 + kk

    def ep_dev(i):
        return {"ep": (ep + i) % NE, "tp": tp}

    def x_dev(i):
        return {"ep": ((x + i) % NX) * 2 + w, "tp": tp}

    def y_dev(i):
        return {"ep": ep, "tp": tp_of((y + i) % NY, z, k)}

    def z_dev(i):
        return {"ep": ep, "tp": tp_of(y, (z + i) % NZ, k)}

    w_dev = {"ep": x * 2 + 1 - w, "tp": tp}
    sib = {"ep": ep, "tp": tp_of(y, z, 1 - k)}
    cross = {"ep": y, "tp": tp_of(ep, z, k)}
    diag = ep == y
    off_diag = jnp.logical_not(diag)

    def remote(src, dst, sems, i, dev):
        return pltpu.make_async_remote_copy(
            src_ref=src,
            dst_ref=dst,
            send_sem=sems.at[0, i],
            recv_sem=sems.at[1, i],
            device_id=dev,
            device_id_type=MESH,
        )

    started = []

    def go(copies):
        for one in copies:
            one.start()
        started.extend(copies)
        return copies

    def arrive(copies):
        for one in copies:
            one.wait_recv()

    def to_y(ref, sems, base=0):
        return go([remote(ref, ref, sems, base + i, y_dev(i)) for i in range(1, NY)])

    def to_z(ref, sems, base=0):
        return go([remote(ref, ref, sems, base + i, z_dev(i)) for i in range(1, NZ)])

    def load(name, dst):
        one = pltpu.make_async_copy(R[name], dst, R.sem_in.at[loads[name]])
        one.start()
        return one

    names = ("table", "count", "gate", "res", "og", "gain", "wg", "wu", "wd", "ctx", "wo")
    loads = {name: i for i, name in enumerate(names)}
    own_cs = R.cs_all.at[x, w]
    ld = {}
    for name in names:
        dst = own_cs.at[pl.ds(0, A)] if name == "ctx" else R[name + "_v"]
        ld[name] = load(name, dst)

    barrier = pltpu.get_barrier_semaphore()
    for i in range(1, NE):
        pl.semaphore_signal(barrier, inc=1, device_id=ep_dev(i), device_id_type=MESH)
    for i in range(1, NY):
        pl.semaphore_signal(barrier, inc=1, device_id=y_dev(i), device_id_type=MESH)
    for i in range(1, NZ):
        pl.semaphore_signal(barrier, inc=1, device_id=z_dev(i), device_id_type=MESH)
    pl.semaphore_signal(barrier, inc=1, device_id=sib, device_id_type=MESH)

    @pl.when(off_diag)
    def _():
        pl.semaphore_signal(barrier, inc=1, device_id=cross, device_id_type=MESH)

    for name in ("table", "count", "gate"):
        ld[name].wait()
    capacity = lax.broadcasted_iota(jnp.int32, (NE, CAP), 1)
    counts = R.count_v[...]
    eyes = lax.broadcasted_iota(jnp.int32, (NE, NE), 0) == lax.broadcasted_iota(
        jnp.int32, (NE, NE), 1
    )
    count_col = jnp.sum(
        jnp.where(eyes, jnp.broadcast_to(counts, (NE, NE)), 0), axis=1, keepdims=True
    )
    table = jnp.where(capacity < count_col, R.table_v[...], -1)

    def spread(values, reps):
        rows = jnp.broadcast_to(values[:, None, :], (NE, reps * CAP, CAP)).reshape(
            NE * reps * CAP, CAP
        )
        row_id = lax.broadcasted_iota(jnp.int32, (NE * reps * CAP, CAP), 0)
        col_id = lax.broadcasted_iota(jnp.int32, (NE * reps * CAP, CAP), 1)
        hit = (row_id % CAP) == col_id
        return jnp.sum(jnp.where(hit, rows, jnp.zeros_like(rows)), axis=1, keepdims=True)

    def one_hot(column):
        lanes = lax.broadcasted_iota(jnp.int32, (column.shape[0], T), 1)
        return jnp.where(column == lanes, 1.0, 0.0).astype(BF)

    is_x = (lax.broadcasted_iota(jnp.int32, (2 * S, 1), 0) // CAP) % 2 == 0
    tokens = spread(table, 2)
    oh_x = one_hot(jnp.where(is_x, tokens, -1))
    oh_go = one_hot(jnp.where(is_x, -1, tokens))
    oh_slot = one_hot(spread(table, 1))
    scale = jnp.where(is_x, 1.0, spread(R.gate_v[...], 2))
    ld["res"].wait()
    ld["og"].wait()
    picked = mm_nt(oh_x, R.res_v[...]) + mm_nt(oh_go, R.og_v[...])
    R.a_send[...] = (scale * picked).astype(BF).reshape(NE, 2 * CAP, FS)

    peers = NE - 1 + NY - 1 + NZ
    pl.semaphore_wait(barrier, jnp.where(diag, peers, peers + 1))

    a_copies = go(
        [
            remote(R.a_send.at[(ep + i) % NE], R.a_recv.at[ep], R.sem_a, i, ep_dev(i))
            for i in range(1, NE)
        ]
    )
    og_cross = remote(R.og_v, R.og_all.at[ep, z, k], R.sem_ogt, 0, cross)

    @pl.when(off_diag)
    def _():
        og_cross.start()

    @pl.when(diag)
    def _():
        R.og_all[ep, z, k] = R.og_v[...]

    R.a_recv[ep] = R.a_send[ep]
    ld["ctx"].wait()
    R.cs_all[x, w, pl.ds(A, S)] = mm_nt(oh_slot, R.cs_all[x, w, pl.ds(0, A)]).astype(BF)
    cs1 = go([remote(own_cs, own_cs, R.sem_cs, 0, w_dev)])
    ld["wo"].wait()
    R.wo_t[...] = R.wo_v[...].T

    for name in ("gain", "wg", "wu", "wd"):
        ld[name].wait()
    arrive(a_copies)
    rows = R.a_recv[...].astype(F32).reshape(NE, 2, CAP, FS)
    rows_x = rows[:, 0].reshape(S, FS)
    rows_go = rows[:, 1].reshape(S, FS)
    gain = R.gain_v[...]
    rows_xg = (rows_x * gain).astype(BF)
    rows_gob = rows_go.astype(BF)
    other = pl.ds(pl.multiple_of((1 - k) * HC, HC), HC)
    own = pl.ds(pl.multiple_of(k * HC, HC), HC)
    lefts = (rows_xg, rows_xg, rows_gob)
    weights = (R.wg_v, R.wu_v, R.wd_v)
    for n in range(3):
        R.part_out[n] = mm(lefts[n], weights[n][:, other]).astype(BF)
    core_copies = go([remote(R.part_out, R.core_recv, R.sem_core, 0, sib)])
    sq_row = col_to_row(jnp.sum(rows_x * rows_x, axis=1, keepdims=True))
    R.tile_sq[0] = jnp.broadcast_to(sq_row, (8, S))
    sqc = go([remote(R.tile_sq.at[0], R.tile_sq_c, R.sem_sqc, 0, sib)])
    for n in range(3):
        R.part_own[n] = mm(lefts[n], weights[n][:, own])

    arrive(core_copies)
    R.part1[...] = (R.part_own[...] + R.core_recv[...].astype(F32)).astype(BF)

    def y_cols(i):
        return pl.ds(pl.multiple_of(((y + i) % NY) * HY, HY), HY)

    def z_rows(i):
        return pl.ds(pl.multiple_of(((z + i) % NZ) * SZ, SZ), SZ)

    zb = go(
        [
            remote(R.part1.at[2, z_rows(i), :], R.zb_recv.at[i - 1], R.sem_zb, i, z_dev(i))
            for i in range(1, NZ)
        ]
    )
    ya = go(
        [
            remote(
                R.part1.at[pl.ds(0, 2), :, y_cols(i)], R.ya_recv.at[i - 1], R.sem_ya, i, y_dev(i)
            )
            for i in range(1, NY)
        ]
    )
    arrive(sqc)
    R.tile_sq[1] = R.tile_sq[0] + R.tile_sq_c[...]
    sqy = go(
        [
            remote(R.tile_sq.at[1], R.tile_sq_y.at[i - 1], R.sem_sqy, i, y_dev(i))
            for i in range(1, NY)
        ]
    )

    @pl.when(off_diag)
    def _():
        og_cross.wait_recv()

    oga1 = to_y(R.og_all.at[y, z, k, pl.ds(0, RA)], R.sem_oga)
    ogb1 = to_z(R.og_all.at[y, z, k, pl.ds(RA, RB)], R.sem_ogb)
    arrive(cs1)
    cs2 = go(
        [remote(R.cs_all.at[x], R.cs_all.at[x], R.sem_cs, i, x_dev(i)) for i in range(1, NX)]
    )

    arrive(zb)
    total = R.part1[2, z_rows(0), :].astype(F32)
    for i in range(1, NZ):
        total = total + R.zb_recv[i - 1].astype(F32)
    R.part2b[...] = total.astype(BF)
    yb = go(
        [
            remote(R.part2b.at[:, y_cols(i)], R.yb_recv.at[i - 1], R.sem_yb, i, y_dev(i))
            for i in range(1, NY)
        ]
    )
    arrive(ya)
    total = R.part1[0:2, :, y_cols(0)].astype(F32)
    for i in range(1, NY):
        total = total + R.ya_recv[i - 1].astype(F32)
    R.part2[...] = total.astype(BF)
    za = go(
        [
            remote(R.part2.at[:, z_rows(i), :], R.za_recv.at[i - 1], R.sem_za, i, z_dev(i))
            for i in range(1, NZ)
        ]
    )
    arrive(sqy)
    sq = R.tile_sq[1]
    for i in range(1, NY):
        sq = sq + R.tile_sq_y[i - 1]
    R.tile_sq[2] = sq
    sqz = go(
        [
            remote(R.tile_sq.at[2], R.tile_sq_z.at[i - 1], R.sem_sqz, i, z_dev(i))
            for i in range(1, NZ)
        ]
    )

    def ring(step):
        half = step == NY // 2
        back = step - 1
        left = R.og_all.at[(y + NY - back) % NY, :, k, pl.ds(RA, RB)]
        right = R.og_all.at[(y + back) % NY, :, k, pl.ds(RA, RB)]
        if half:
            left = R.og_all.at[(y + NY - back) % NY, :, k, pl.ds(RA, RB), pl.ds(0, TH)]
            right = R.og_all.at[(y + back) % NY, :, k, pl.ds(RA, RB), pl.ds(TH, TH)]
        return go(
            [
                remote(left, left, R.sem_ring, 2 * step, y_dev(1)),
                remote(right, right, R.sem_ring, 2 * step + 1, y_dev(NY - 1)),
            ]
        )

    arrive(ogb1)
    hop = ring(1)

    arrive(sqz)
    sq = R.tile_sq[2]
    for i in range(1, NZ):
        sq = sq + R.tile_sq_z[i - 1]
    inv_col = row_to_col(lax.rsqrt(sq[0:1] / D + norm_eps))
    R.inv_buf[...] = jnp.broadcast_to(inv_col, (S, HY))
    arrive(yb)
    hid_grad = R.part2b[:, y_cols(0)].astype(F32)
    for i in range(1, NY):
        hid_grad = hid_grad + R.yb_recv[i - 1].astype(F32)
    arrive(za)
    total = R.part2[:, z_rows(0), :].astype(F32)
    for i in range(1, NZ):
        total = total + R.za_recv[i - 1].astype(F32)
    inv_mine = R.inv_buf[z_rows(0), :]
    pre_gate = inv_mine * total[0]
    pre_up = inv_mine * total[1]
    sigmoid_gate = jax.nn.sigmoid(pre_gate)
    silu_gate = pre_gate * sigmoid_gate
    hidden = (silu_gate * pre_up).astype(BF)
    d_gate = (hid_grad * pre_up * sigmoid_gate * (1.0 + pre_gate * (1.0 - sigmoid_gate))).astype(BF)
    d_up = (hid_grad * silu_gate).astype(BF)
    my_cols = pl.ds(pl.multiple_of(k * HC + y * HY, HY), HY)
    R.act[0, z_rows(0), my_cols] = d_gate
    R.act[1, z_rows(0), my_cols] = d_up
    R.act[2, z_rows(0), my_cols] = hidden

    g1 = to_z(R.act.at[0, z_rows(0), my_cols], R.sem_g1)
    u1 = to_y(R.act.at[1, z_rows(0), my_cols], R.sem_u1)
    h1 = to_z(R.act.at[2, z_rows(0), my_cols], R.sem_h1)
    dots = jnp.sum(d_gate.astype(F32) * pre_gate + d_up.astype(F32) * pre_up, axis=1, keepdims=True)
    R.dot_buf[...] = jnp.zeros_like(R.dot_buf)
    R.dot_buf[z_rows(0), :] = jnp.broadcast_to(dots, (SZ, 128))
    R.tile_dot[0] = jnp.broadcast_to(col_to_row(R.dot_buf[:, 0:1]), (8, S))
    dtz = go(
        [
            remote(R.tile_dot.at[0], R.tile_dot_z.at[i - 1], R.sem_dtz, i, z_dev(i))
            for i in range(1, NZ)
        ]
    )
    arrive(g1)
    g2 = to_y(R.act.at[0, :, my_cols], R.sem_g2)
    arrive(u1)
    u2 = to_z(R.act.at[1, z_rows(0), own], R.sem_u2)
    arrive(dtz)
    dt = R.tile_dot[0]
    for i in range(1, NZ):
        dt = dt + R.tile_dot_z[i - 1]
    R.tile_dot[1] = dt
    dty = go(
        [
            remote(R.tile_dot.at[1], R.tile_dot_y.at[i - 1], R.sem_dty, i, y_dev(i))
            for i in range(1, NY)
        ]
    )
    arrive(oga1)
    oga2 = to_z(R.og_all.at[:, z, k, pl.ds(0, RA)], R.sem_oga, NY)
    steps = NY // 2
    if steps >= 2:
        arrive(hop)
        hop = ring(2)

    arrive(g2)
    arrive(u2)
    own_act = R.act.at[pl.ds(0, 2), :, own]
    gk = go([remote(own_act, own_act, R.sem_gk, 0, sib)])
    arrive(h1)
    h2 = to_y(R.act.at[2, :, my_cols], R.sem_h2)
    arrive(dty)
    dt = R.tile_dot[1]
    for i in range(1, NY):
        dt = dt + R.tile_dot_y[i - 1]
    R.tile_dot[2] = dt
    dtc = go([remote(R.tile_dot.at[2], R.tile_dot_c, R.sem_dtc, 0, sib)])
    inv_col = R.inv_buf[:, 0:1]
    normed = rows_x * inv_col
    arrive(dtc)
    dots_col = row_to_col((R.tile_dot[2] + R.tile_dot_c[...])[0:1])
    arrive(gk)
    slot_back = (
        (mm_nt(R.act[0], R.wg_v[...]) + mm_nt(R.act[1], R.wu_v[...])).astype(BF).astype(F32)
    )
    delta = inv_col * (gain * slot_back - normed * (dots_col / D))
    R.delta_own[...] = delta.astype(BF)

    d_cross = remote(R.delta_own, R.delta_all.at[z, k, ep], R.sem_dt, 0, cross)

    @pl.when(off_diag)
    def _():
        d_cross.start()

    @pl.when(diag)
    def _():
        R.delta_all[z, k, ep] = R.delta_own[...]

    R.ret_send[...] = delta.reshape(NE, CAP, FS)
    R.ret_recv[ep] = R.ret_send[ep]
    ret_copies = go(
        [
            remote(R.ret_send.at[(ep + i) % NE], R.ret_recv.at[ep], R.sem_ret, i, ep_dev(i))
            for i in range(1, NE)
        ]
    )
    if steps >= 3:
        arrive(hop)
        hop = ring(3)
    slot_in = (normed * gain).astype(BF)
    R.gate_out[...] = mm_tn(slot_in, R.act[0]).astype(BF)

    @pl.when(off_diag)
    def _():
        d_cross.wait_recv()

    da1 = to_y(R.delta_all.at[z, k, y, pl.ds(0, SH)], R.sem_da)
    db1 = to_z(R.delta_all.at[z, k, y, pl.ds(SH, SH)], R.sem_db)
    arrive(h2)
    own_hid = R.act.at[2, :, own]
    hk = go([remote(own_hid, own_hid, R.sem_gk, 1, sib)])
    if steps >= 4:
        arrive(hop)
        hop = ring(4)
    R.up_out[...] = mm_tn(slot_in, R.act[1]).astype(BF)
    arrive(db1)
    db2 = to_y(R.delta_all.at[:, k, y, pl.ds(SH, SH)], R.sem_db, NZ)
    arrive(da1)
    da2 = to_z(R.delta_all.at[z, k, :, pl.ds(0, SH)], R.sem_da, NY)

    arrive(hop)
    arrive(oga2)
    ogk_mine = R.og_all.at[:, :, k]
    ogk = go([remote(ogk_mine, ogk_mine, R.sem_ogk, 0, sib)])
    arrive(hk)
    R.down_out[...] = mm_tn(rows_gob, R.act[2]).astype(BF)
    arrive(ogk)
    for g in range(NE):
        block = R.og_all[g].reshape(BL, T)
        R.base_send[g // 2, g % 2] = mm(R.wo_t[...], block).astype(BF)
    bx = go(
        [
            remote(R.base_send.at[(x + i) % NX], R.bx_recv.at[i - 1], R.sem_bx, i, x_dev(i))
            for i in range(1, NX)
        ]
    )
    arrive(da2)
    arrive(db2)
    dk_mine = R.delta_all.at[:, k]
    dk = go([remote(dk_mine, dk_mine, R.sem_dk, 0, sib)])
    arrive(cs2)
    for g in range(NE):
        one = mm_nt(R.og_all[g].reshape(BL, T), R.cs_all[g // 2, g % 2, pl.ds(0, A)])
        if g == 0:
            R.wo_acc[...] = one
        else:
            R.wo_acc[...] += one
    sel = R.cs_all[:, :, pl.ds(A, S)].astype(F32).reshape(NE, NE, CAP, A)
    for e in range(NE):
        R.sel_perm[e] = sel[:, e].reshape(S, A).astype(BF)

    arrive(dk)
    slots = None
    for q in range(NZ * 2):
        block = R.delta_all[q // 2, q % 2].reshape(NE * S, FS)
        one = mm(block, R.wo_v[pl.ds(q * FS, FS), :])
        slots = one if slots is None else slots + one
    slots = slots.reshape(NE, NE, CAP, A)
    for g in range(NE):
        R.msg_send[g] = slots[:, g].reshape(S, A).astype(BF)
    msg_copies = go(
        [
            remote(R.msg_send.at[(ep + i) % NE], R.msg_recv.at[ep], R.sem_msg, i, ep_dev(i))
            for i in range(1, NE)
        ]
    )
    R.msg_recv[ep] = R.msg_send[ep]
    arrive(bx)
    total = R.base_send[x].astype(F32)
    for i in range(1, NX):
        total = total + R.bx_recv[i - 1].astype(F32)
    R.base_two[...] = total.astype(BF)
    bw = go([remote(R.base_two.at[1 - w], R.bw_recv, R.sem_bx, 0, w_dev)])
    right = R.sel_perm[...].reshape(NE * S, A)
    for q in range(NZ * 2):
        feats = pl.ds(q * FS, FS)
        block = R.delta_all[q // 2, q % 2].reshape(NE * S, FS)
        R.wo_out[feats, :] = (R.wo_acc[feats, :] + mm_tn(block, right)).astype(BF)

    arrive(ret_copies)
    returned = R.ret_recv[...].reshape(S, FS).astype(BF)
    R.resid_out[...] = (R.og_v[...].astype(F32) + mm_tn(returned, oh_slot)).astype(BF)

    arrive(msg_copies)
    picked = R.msg_recv[0].astype(F32)
    for i in range(1, NE):
        picked = picked + R.msg_recv[i].astype(F32)
    slot_part = mm_tn(picked.astype(BF), oh_slot)
    arrive(bw)
    total = R.base_two[w].astype(F32) + R.bw_recv[...].astype(F32)
    R.ctx_out[...] = (total + slot_part).astype(BF)

    for one in started:
        one.wait_send()

    @pl.when(off_diag)
    def _():
        og_cross.wait_send()
        d_cross.wait_send()


class Refs:
    def __init__(self, names, refs):
        self.refs = dict(zip(names, refs, strict=True))

    def __getattr__(self, name):
        return self.refs[name]

    def __getitem__(self, name):
        return self.refs[name]


def copy_out(*refs):
    half = (len(refs) - 1) // 2
    sems = refs[-1]
    copies = [
        pltpu.make_async_copy(refs[i], refs[half + i], sems.at[i]) for i in range(half)
    ]
    for one in copies:
        one.start()
    for one in copies:
        one.wait()


def shards(
    dims,
    residual,
    out_grad,
    norm_gain,
    context,
    w_out,
    w_gate,
    w_up,
    w_down,
    slot_token,
    slot_count,
    slot_gate,
):
    NE, NY, NZ, CAP, FS, T, A, H, D = dims
    NX = NE // 2
    S = NE * CAP
    BL = NZ * 2 * FS
    HC = H // 2
    HY = HC // NY
    SZ = S // NZ
    V = pltpu.VMEM
    dma = pltpu.SemaphoreType.DMA
    hbm = pl.BlockSpec(memory_space=pltpu.HBM)
    vmem = pl.BlockSpec(memory_space=pltpu.VMEM)
    inputs = dict(
        table=slot_token[0],
        count=slot_count,
        gate=slot_gate[0],
        res=residual[0],
        og=out_grad[0],
        gain=norm_gain.reshape(1, FS),
        ctx=context[0],
        wo=w_out,
        wg=w_gate[0],
        wu=w_up[0],
        wd=w_down[0],
    )
    outs = dict(
        resid_out=(FS, T),
        ctx_out=(A, T),
        wo_out=(BL, A),
        gate_out=(FS, H),
        up_out=(FS, H),
        down_out=(FS, H),
    )
    scratch = dict(
        table_v=V((NE, CAP), jnp.int32),
        count_v=V((1, NE), jnp.int32),
        gate_v=V((NE, CAP), F32),
        res_v=V((FS, T), BF),
        og_v=V((FS, T), BF),
        gain_v=V((1, FS), F32),
        wo_v=V((BL, A), BF),
        wo_t=V((A, BL), BF),
        wg_v=V((FS, H), BF),
        wu_v=V((FS, H), BF),
        wd_v=V((FS, H), BF),
        a_send=V((NE, 2 * CAP, FS), BF),
        a_recv=V((NE, 2 * CAP, FS), BF),
        og_all=V((NE, NZ, 2, FS, T), BF),
        cs_all=V((NX, 2, A + S, T), BF),
        sel_perm=V((NE, S, A), BF),
        part_out=V((3, S, HC), BF),
        part_own=V((3, S, HC), F32),
        core_recv=V((3, S, HC), BF),
        part1=V((3, S, HC), BF),
        ya_recv=V((NY - 1, 2, S, HY), BF),
        part2=V((2, S, HY), BF),
        za_recv=V((max(NZ - 1, 1), 2, SZ, HY), BF),
        zb_recv=V((max(NZ - 1, 1), SZ, HC), BF),
        part2b=V((SZ, HC), BF),
        yb_recv=V((NY - 1, SZ, HY), BF),
        tile_sq=V((3, 8, S), F32),
        tile_sq_c=V((8, S), F32),
        tile_sq_y=V((NY - 1, 8, S), F32),
        tile_sq_z=V((max(NZ - 1, 1), 8, S), F32),
        tile_dot=V((3, 8, S), F32),
        tile_dot_c=V((8, S), F32),
        tile_dot_y=V((NY - 1, 8, S), F32),
        tile_dot_z=V((max(NZ - 1, 1), 8, S), F32),
        inv_buf=V((S, HY), F32),
        dot_buf=V((S, 128), F32),
        act=V((3, S, H), BF),
        ret_send=V((NE, CAP, FS), F32),
        ret_recv=V((NE, CAP, FS), F32),
        delta_own=V((S, FS), BF),
        delta_all=V((NZ, 2, NE, S, FS), BF),
        base_send=V((NX, 2, A, T), BF),
        bx_recv=V((max(NX - 1, 1), 2, A, T), BF),
        base_two=V((2, A, T), BF),
        bw_recv=V((A, T), BF),
        wo_acc=V((BL, A), F32),
        msg_send=V((NE, S, A), BF),
        msg_recv=V((NE, S, A), BF),
        sem_in=dma((11,)),
        sem_a=dma((2, NE)),
        sem_ogt=dma((2, 1)),
        sem_oga=dma((2, NY + NZ)),
        sem_ogb=dma((2, NZ)),
        sem_ring=dma((2, NY + 2)),
        sem_ogk=dma((2, 1)),
        sem_cs=dma((2, max(NX, 1))),
        sem_core=dma((2, 1)),
        sem_ya=dma((2, NY)),
        sem_za=dma((2, NZ)),
        sem_yb=dma((2, NY)),
        sem_zb=dma((2, NZ)),
        sem_sqc=dma((2, 1)),
        sem_sqy=dma((2, NY)),
        sem_sqz=dma((2, NZ)),
        sem_dtc=dma((2, 1)),
        sem_dty=dma((2, NY)),
        sem_dtz=dma((2, NZ)),
        sem_g1=dma((2, NZ)),
        sem_u1=dma((2, NY)),
        sem_h1=dma((2, NZ)),
        sem_g2=dma((2, NY)),
        sem_u2=dma((2, NZ)),
        sem_h2=dma((2, NY)),
        sem_gk=dma((2, 2)),
        sem_ret=dma((2, NE)),
        sem_dt=dma((2, 1)),
        sem_da=dma((2, NY + NZ)),
        sem_db=dma((2, NY + NZ)),
        sem_dk=dma((2, 1)),
        sem_bx=dma((2, max(NX, 1))),
        sem_msg=dma((2, NE)),
    )
    spec = tuple(inputs) + tuple(outs) + tuple(scratch)
    out_shape = tuple(jax.ShapeDtypeStruct(shape, BF) for shape in outs.values())
    results = pl.pallas_call(
        functools.partial(kernel, dims, spec),
        out_shape=out_shape,
        in_specs=[hbm] * len(inputs),
        out_specs=[vmem] * len(outs),
        scratch_shapes=list(scratch.values()),
        compiler_params=pltpu.CompilerParams(
            collective_id=0, has_side_effects=True, vmem_limit_bytes=48 * 1024 * 1024
        ),
    )(*inputs.values())
    resid, ctx_grad, wo_grad, gate_grad, up_grad, down_grad = pl.pallas_call(
        copy_out,
        out_shape=out_shape,
        in_specs=[vmem] * len(outs),
        out_specs=[hbm] * len(outs),
        scratch_shapes=[dma((len(outs),))],
    )(*results)
    return (
        resid[None],
        ctx_grad[None],
        wo_grad,
        gate_grad[None],
        up_grad[None],
        down_grad[None],
    )


def solution(mesh):
    sizes = dict(mesh.shape)
    NE = sizes["ep"]
    NY = NE
    NZ = sizes["tp"] // (2 * NY)

    def run(residual, out_grad, norm_gain, context, w_out, w_gate, w_up, w_down, *slots):
        D, T = residual.shape[1:]
        dims = (
            NE,
            NY,
            NZ,
            slots[0].shape[2],
            D // sizes["tp"],
            T,
            context.shape[1] // sizes["tp"],
            w_gate.shape[2],
            D,
        )
        return jax.shard_map(
            functools.partial(shards, dims),
            mesh=mesh,
            in_specs=(
                P("ep", "tp", None),
                P("ep", "tp", None),
                P("tp"),
                P("ep", "tp", None),
                P("ep", "tp"),
                P("ep", "tp", None),
                P("ep", "tp", None),
                P("ep", "tp", None),
                P("ep", None, None),
                P("ep", None),
                P("ep", None, None),
            ),
            out_specs=(
                P("ep", "tp", None),
                P("ep", "tp", None),
                P("ep", "tp"),
                P("ep", "tp", None),
                P("ep", "tp", None),
                P("ep", "tp", None),
            ),
            check_vma=False,
        )(residual, out_grad, norm_gain, context, w_out, w_gate, w_up, w_down, *slots)

    return run
```

time: 1150 us -> 113 us (0.10)
  waiting for transfers between devices: 791 us -> 0 us
  blocking collectives: 295 us -> 0 us
  Pallas kernels: 0 us -> 100 us
  matrix products: 21.1 us -> 0 us
  starting transfers between devices: 14.1 us -> 0 us
  between operations: 13.9 us -> 0.7 us
    psum x1 -> x0, waiting for transfers between devices: 561 us -> none  [shards(): pre_gate, pre_up, hid_grad = lax.psum((gate_part, up_part, hid_part), 'tp')]
    psum x2 -> x0, blocking collectives: 286 us -> none  [the longest x1 146 us: shards(): square = lax.psum(jnp.sum(stream * stream, axis=0), 'tp')]
    all_gather x3 -> x0, waiting for transfers between devices: 224 us -> none  [the longest x1 109 us: shards(): lax.all_gather(w_out, 'ep', axis=0, tiled=True)]
    pallas_call x0 -> x2, Pallas kernels: none -> 100 us  [the longest x1 97.4 us: shards(): pl.pallas_call(functools.partial(kernel, dims, spec), out_shape=out_shape...]
    dot_general x13 -> x0, matrix products: 21.1 us -> none  [the longest x4 9.47 us: contract_rows(): lax.dot_general(left, right, (((0,), (0,)), ((), ())), preferred_element_...]
    all_to_all x3 -> x0, starting transfers between devices: 14 us -> none  [the longest x1 5.7 us: shards(): lax.all_to_all(full_grad, 'ep', split_axis=0, concat_axis=1, tiled=True)]
  transfers between devices with their start and end apart: 7 -> 0, of which waited for: 6 -> 0; matrix products, arithmetic and copies ran while one was open for 2% -> 0% of each run, Pallas kernels for 0% -> 0%
where the time goes in v2:
time: 113 us
  Pallas kernels  100 us (88%)
  local copies, waits for them, and re-layouts  11.6 us (10%)
    pallas_call x1, Pallas kernels, shards(): pl.pallas_call(functools.partial(kernel, dims, spec), out_shape=out_shape...  97.4 us
    unnamed x34, local copies, waits for them, and re-layouts  11.6 us
    pallas_call x1, Pallas kernels, shards(): pl.pallas_call(copy_out, out_shape=out_shape, in_specs=[vmem] * len(outs)...  2.86 us

profile of v2, /device:TPU:1, one launch (start us, length us, event | category | flops | bytes accessed | tf_op | source)
XLA Modules:
  0.0 112.6 jit_solution(18306445284575506033)
XLA Ops:
  0.6 0.0 copy-start.14
  0.6 0.0 copy-start.13
  0.7 0.0 copy-start.15
  0.7 0.0 copy-start.16
  0.7 0.6 copy-done.14
  1.3 0.0 copy-done.13
  1.3 0.0 copy-done.15
  1.3 0.0 copy-done.16
  1.3 0.0 copy-start
  1.3 1.0 copy-done
  2.4 0.0 copy-start.1
  2.4 1.0 copy-done.1
  3.4 0.0 copy-start.2
  3.4 1.0 copy-done.2
  4.4 0.0 copy-start.3
  4.4 1.0 copy-done.3
  5.4 0.0 copy-start.9
  5.4 0.9 copy-done.9
  6.3 0.0 copy-start.11
  6.3 0.8 copy-done.11
  7.1 0.0 copy-start.12
  7.1 0.8 copy-done.12
  8.0 97.4 %shard_map.154 = (bf16[112,256]{1,0:T(8,128)(2,1)S(1)}, bf16[256,256]{1,0:T(8,128)(2,1)S(1)}, bf16[896,256]{1,0:T(8,128)(2,1)S(1)}, bf16[112,2048]{1,0:T(8,128)(...) custom-call(s32[8,8]{1,0:T(8,128)S(1)} %bitcast.20, s32[1,8]{1,0:T(1,128)S(1)} %copy-done.15, ...), custom_call_target="tpu_custom_call" | custom-call | tf_op jit(solution)/shard_map/pallas_call | solution.py:693
  105.4 0.0 copy-start.4
  105.4 0.8 copy-done.4
  106.2 0.0 copy-start.5
  106.2 0.8 copy-done.5
  106.9 0.8 copy-done.6
  107.7 0.8 copy-done.7
  108.5 0.7 copy-done.8
  109.2 0.6 copy-done.10
  109.8 2.9 %shard_map.155 = (bf16[112,256]{1,0:T(8,128)(2,1)}, bf16[256,256]{1,0:T(8,128)(2,1)}, bf16[896,256]{1,0:T(8,128)(2,1)}, bf16[112,2048]{1,0:T(8,128)(2,1)}, bf16[...) custom-call(bf16[112,256]{1,0:T(8,128)(2,1)} %copy-done.10, bf16[256,256]{1,0:T(8,128)(2,1)} %copy-done.8, ...), custom_call_target="tpu_custom_call" | custom-call | tf_op jit(solution)/shard_map/pallas_call | solution.py:703
  (4 shorter events, 0.0 us)
Async XLA Ops:
  0.6 0.7 copy-start.14
  0.6 0.7 copy-start.13
  0.7 0.7 copy-start.15
  0.7 0.7 copy-start.16
  1.3 1.0 copy-start
  2.4 1.0 copy-start.1
  3.4 1.0 copy-start.2
  4.4 1.0 copy-start.3
  5.4 0.9 copy-start.9
  6.3 0.8 copy-start.11
  7.1 0.8 copy-start.12
  105.4 0.8 copy-start.4
  106.2 0.8 copy-start.5
  106.9 0.8 copy-start.6
  107.7 0.8 copy-start.7
  108.5 0.7 copy-start.8
  109.1 0.6 copy-start.10

commit v3 on v2

--- a/solution.py
+++ b/solution.py
@@ -135,6 +135,18 @@
     for name in names:
         dst = own_cs.at[pl.ds(0, A)] if name == "ctx" else R[name + "_v"]
         ld[name] = load(name, dst)
+
+    outs = ("resid_out", "ctx_out", "wo_out", "gate_out", "up_out", "down_out")
+    stores = []
+
+    def store(name, value):
+        R[name + "_v"][...] = value
+        stored(name)
+
+    def stored(name):
+        one = pltpu.make_async_copy(R[name + "_v"], R[name], R.sem_out.at[outs.index(name)])
+        one.start()
+        stores.append(one)
 
     barrier = pltpu.get_barrier_semaphore()
     for i in range(1, NE):
@@ -435,7 +447,7 @@
         arrive(hop)
         hop = ring(3)
     slot_in = (normed * gain).astype(BF)
-    R.gate_out[...] = mm_tn(slot_in, R.act[0]).astype(BF)
+    store("gate_out", mm_tn(slot_in, R.act[0]).astype(BF))
 
     @pl.when(off_diag)
     def _():
@@ -449,7 +461,7 @@
     if steps >= 4:
         arrive(hop)
         hop = ring(4)
-    R.up_out[...] = mm_tn(slot_in, R.act[1]).astype(BF)
+    store("up_out", mm_tn(slot_in, R.act[1]).astype(BF))
     arrive(db1)
     db2 = to_y(R.delta_all.at[:, k, y, pl.ds(SH, SH)], R.sem_db, NZ)
     arrive(da1)
@@ -460,7 +472,7 @@
     ogk_mine = R.og_all.at[:, :, k]
     ogk = go([remote(ogk_mine, ogk_mine, R.sem_ogk, 0, sib)])
     arrive(hk)
-    R.down_out[...] = mm_tn(rows_gob, R.act[2]).astype(BF)
+    store("down_out", mm_tn(rows_gob, R.act[2]).astype(BF))
     arrive(ogk)
     for g in range(NE):
         block = R.og_all[g].reshape(BL, T)
@@ -512,11 +524,12 @@
     for q in range(NZ * 2):
         feats = pl.ds(q * FS, FS)
         block = R.delta_all[q // 2, q % 2].reshape(NE * S, FS)
-        R.wo_out[feats, :] = (R.wo_acc[feats, :] + mm_tn(block, right)).astype(BF)
+        R.wo_out_v[feats, :] = (R.wo_acc[feats, :] + mm_tn(block, right)).astype(BF)
+    stored("wo_out")
 
     arrive(ret_copies)
     returned = R.ret_recv[...].reshape(S, FS).astype(BF)
-    R.resid_out[...] = (R.og_v[...].astype(F32) + mm_tn(returned, oh_slot)).astype(BF)
+    store("resid_out", (R.og_v[...].astype(F32) + mm_tn(returned, oh_slot)).astype(BF))
 
     arrive(msg_copies)
     picked = R.msg_recv[0].astype(F32)
@@ -525,10 +538,12 @@
     slot_part = mm_tn(picked.astype(BF), oh_slot)
     arrive(bw)
     total = R.base_two[w].astype(F32) + R.bw_recv[...].astype(F32)
-    R.ctx_out[...] = (total + slot_part).astype(BF)
+    store("ctx_out", (total + slot_part).astype(BF))
 
     for one in started:
         one.wait_send()
+    for one in stores:
+        one.wait()
 
     @pl.when(off_diag)
     def _():
@@ -548,14 +563,21 @@
 
 
 def copy_out(*refs):
-    half = (len(refs) - 1) // 2
+    count = (len(refs) - 1) // 3
+    sources, targets, held = refs[:count], refs[count : 2 * count], refs[2 * count : -1]
     sems = refs[-1]
-    copies = [
-        pltpu.make_async_copy(refs[i], refs[half + i], sems.at[i]) for i in range(half)
+    loads = [
+        pltpu.make_async_copy(sources[i], held[i], sems.at[0, i]) for i in range(count)
     ]
-    for one in copies:
+    stores = [
+        pltpu.make_async_copy(held[i], targets[i], sems.at[1, i]) for i in range(count)
+    ]
+    for one in loads:
         one.start()
-    for one in copies:
+    for load, one in zip(loads, stores, strict=True):
+        load.wait()
+        one.start()
+    for one in stores:
         one.wait()
 
 
@@ -583,7 +605,6 @@
     V = pltpu.VMEM
     dma = pltpu.SemaphoreType.DMA
     hbm = pl.BlockSpec(memory_space=pltpu.HBM)
-    vmem = pl.BlockSpec(memory_space=pltpu.VMEM)
     inputs = dict(
         table=slot_token[0],
         count=slot_count,
@@ -654,7 +675,14 @@
         wo_acc=V((BL, A), F32),
         msg_send=V((NE, S, A), BF),
         msg_recv=V((NE, S, A), BF),
+        resid_out_v=V((FS, T), BF),
+        ctx_out_v=V((A, T), BF),
+        wo_out_v=V((BL, A), BF),
+        gate_out_v=V((FS, H), BF),
+        up_out_v=V((FS, H), BF),
+        down_out_v=V((FS, H), BF),
         sem_in=dma((11,)),
+        sem_out=dma((6,)),
         sem_a=dma((2, NE)),
         sem_ogt=dma((2, 1)),
         sem_oga=dma((2, NY + NZ)),
@@ -694,18 +722,19 @@
         functools.partial(kernel, dims, spec),
         out_shape=out_shape,
         in_specs=[hbm] * len(inputs),
-        out_specs=[vmem] * len(outs),
+        out_specs=[hbm] * len(outs),
         scratch_shapes=list(scratch.values()),
         compiler_params=pltpu.CompilerParams(
-            collective_id=0, has_side_effects=True, vmem_limit_bytes=48 * 1024 * 1024
+            collective_id=0, has_side_effects=True, vmem_limit_bytes=62 * 1024 * 1024
         ),
     )(*inputs.values())
     resid, ctx_grad, wo_grad, gate_grad, up_grad, down_grad = pl.pallas_call(
         copy_out,
         out_shape=out_shape,
-        in_specs=[vmem] * len(outs),
+        in_specs=[hbm] * len(outs),
         out_specs=[hbm] * len(outs),
-        scratch_shapes=[dma((len(outs),))],
+        scratch_shapes=[V(shape, BF) for shape in outs.values()] + [dma((2, len(outs)))],
+        compiler_params=pltpu.CompilerParams(vmem_limit_bytes=62 * 1024 * 1024),
     )(*results)
     return (
         resid[None],

time: 113 us -> 99.5 us (0.88)
  the two profiles are of different devices: /device:TPU:1 before, /device:TPU:72 now
where the time goes in v3:
time: 99.5 us; the launch traced here: 99.4 us
  Pallas kernels  98.7 us (99%)
    pallas_call x1, Pallas kernels, shards(): pl.pallas_call(functools.partial(kernel, dims, spec), out_shape=out_shape...  96.3 us
    pallas_call x1, Pallas kernels, shards(): pl.pallas_call(copy_out, out_shape=out_shape, in_specs=[hbm] * len(outs),...  2.44 us

profile of v3, /device:TPU:72, one launch (start us, length us, event | category | flops | bytes accessed | tf_op | source)
XLA Modules:
  0.0 99.4 jit_solution(3906385793071645813)
XLA Ops:
  0.6 96.3 %shard_map.154 = (bf16[112,256]{1,0:T(8,128)(2,1)}, bf16[256,256]{1,0:T(8,128)(2,1)}, bf16[896,256]{1,0:T(8,128)(2,1)}, bf16[112,2048]{1,0:T(8,128)(2,1)}, bf16[...) custom-call(s32[8,8]{1,0:T(8,128)} %bitcast.20, s32[1,8]{1,0:T(1,128)} %refs_1_.1, f32[8,8]{1,0:T(8,128)} %bitcast.21, ...), custom_call_target="tpu_custom_call" | custom-call | tf_op jit(solution)/shard_map/pallas_call | solution.py:721
  96.9 2.4 %shard_map.155 = (bf16[112,256]{1,0:T(8,128)(2,1)}, bf16[256,256]{1,0:T(8,128)(2,1)}, bf16[896,256]{1,0:T(8,128)(2,1)}, bf16[112,2048]{1,0:T(8,128)(2,1)}, bf16[...) custom-call(bf16[112,256]{1,0:T(8,128)(2,1)} %get-tuple-element.18.refs_0_, bf16[256,256]{1,0:T(8,128)(2,1)} %get-tuple-element.19.refs_1_, ...), custom_call_target="tpu_custom_call" | custom-call | tf_op jit(solution)/shard_map/pallas_call | solution.py:731

commit v4 on v3

--- a/solution.py
+++ b/solution.py
@@ -60,10 +60,11 @@
     HY = HC // NY
     TH = T // 2
     SH = S // 2
-    RA = 32
-    RB = FS - RA
     BL = NZ * 2 * FS
     R = Refs(spec, refs)
+    far_y = sorted(range(1, NY), key=lambda i: -min(i, NY - i))
+    far_z = sorted(range(1, NZ), key=lambda i: -min(i, NZ - i))
+    far_e = sorted(range(1, NE), key=lambda i: -min(i // 2, NX - i // 2))
 
     ep = lax.axis_index("ep")
     tp = lax.axis_index("tp")
@@ -92,6 +93,7 @@
     w_dev = {"ep": x * 2 + 1 - w, "tp": tp}
     sib = {"ep": ep, "tp": tp_of(y, z, 1 - k)}
     cross = {"ep": y, "tp": tp_of(ep, z, k)}
+
     diag = ep == y
     off_diag = jnp.logical_not(diag)
 
@@ -118,10 +120,15 @@
             one.wait_recv()
 
     def to_y(ref, sems, base=0):
-        return go([remote(ref, ref, sems, base + i, y_dev(i)) for i in range(1, NY)])
+        return go([remote(ref, ref, sems, base + i, y_dev(i)) for i in far_y])
 
     def to_z(ref, sems, base=0):
-        return go([remote(ref, ref, sems, base + i, z_dev(i)) for i in range(1, NZ)])
+        return go([remote(ref, ref, sems, base + i, z_dev(i)) for i in far_z])
+
+    def arrive_whole(one):
+        @pl.when(off_diag)
+        def _():
+            one.wait_recv()
 
     def load(name, dst):
         one = pltpu.make_async_copy(R[name], dst, R.sem_in.at[loads[name]])
@@ -149,13 +156,14 @@
         stores.append(one)
 
     barrier = pltpu.get_barrier_semaphore()
-    for i in range(1, NE):
+    for i in far_e:
         pl.semaphore_signal(barrier, inc=1, device_id=ep_dev(i), device_id_type=MESH)
-    for i in range(1, NY):
+    for i in far_y:
         pl.semaphore_signal(barrier, inc=1, device_id=y_dev(i), device_id_type=MESH)
-    for i in range(1, NZ):
+    for i in far_z:
         pl.semaphore_signal(barrier, inc=1, device_id=z_dev(i), device_id_type=MESH)
     pl.semaphore_signal(barrier, inc=1, device_id=sib, device_id_type=MESH)
+
 
     @pl.when(off_diag)
     def _():
@@ -203,10 +211,10 @@
     a_copies = go(
         [
             remote(R.a_send.at[(ep + i) % NE], R.a_recv.at[ep], R.sem_a, i, ep_dev(i))
-            for i in range(1, NE)
-        ]
-    )
-    og_cross = remote(R.og_v, R.og_all.at[ep, z, k], R.sem_ogt, 0, cross)
+            for i in far_e
+        ]
+    )
+    og_cross = remote(R.og_v, R.og_all.at[ep, z, k], R.sem_oga, 0, cross)
 
     @pl.when(off_diag)
     def _():
@@ -217,16 +225,13 @@
         R.og_all[ep, z, k] = R.og_v[...]
 
     R.a_recv[ep] = R.a_send[ep]
-    ld["ctx"].wait()
-    R.cs_all[x, w, pl.ds(A, S)] = mm_nt(oh_slot, R.cs_all[x, w, pl.ds(0, A)]).astype(BF)
-    cs1 = go([remote(own_cs, own_cs, R.sem_cs, 0, w_dev)])
-    ld["wo"].wait()
-    R.wo_t[...] = R.wo_v[...].T
 
     for name in ("gain", "wg", "wu", "wd"):
         ld[name].wait()
     arrive(a_copies)
     rows = R.a_recv[...].astype(F32).reshape(NE, 2, CAP, FS)
+    arrive_whole(og_cross)
+    ogb1 = to_z(R.og_all.at[y, z, k], R.sem_ogb)
     rows_x = rows[:, 0].reshape(S, FS)
     rows_go = rows[:, 1].reshape(S, FS)
     gain = R.gain_v[...]
@@ -257,7 +262,7 @@
     zb = go(
         [
             remote(R.part1.at[2, z_rows(i), :], R.zb_recv.at[i - 1], R.sem_zb, i, z_dev(i))
-            for i in range(1, NZ)
+            for i in far_z
         ]
     )
     ya = go(
@@ -265,7 +270,7 @@
             remote(
                 R.part1.at[pl.ds(0, 2), :, y_cols(i)], R.ya_recv.at[i - 1], R.sem_ya, i, y_dev(i)
             )
-            for i in range(1, NY)
+            for i in far_y
         ]
     )
     arrive(sqc)
@@ -273,63 +278,18 @@
     sqy = go(
         [
             remote(R.tile_sq.at[1], R.tile_sq_y.at[i - 1], R.sem_sqy, i, y_dev(i))
-            for i in range(1, NY)
-        ]
-    )
-
-    @pl.when(off_diag)
-    def _():
-        og_cross.wait_recv()
-
-    oga1 = to_y(R.og_all.at[y, z, k, pl.ds(0, RA)], R.sem_oga)
-    ogb1 = to_z(R.og_all.at[y, z, k, pl.ds(RA, RB)], R.sem_ogb)
-    arrive(cs1)
-    cs2 = go(
-        [remote(R.cs_all.at[x], R.cs_all.at[x], R.sem_cs, i, x_dev(i)) for i in range(1, NX)]
-    )
-
-    arrive(zb)
-    total = R.part1[2, z_rows(0), :].astype(F32)
-    for i in range(1, NZ):
-        total = total + R.zb_recv[i - 1].astype(F32)
-    R.part2b[...] = total.astype(BF)
-    yb = go(
-        [
-            remote(R.part2b.at[:, y_cols(i)], R.yb_recv.at[i - 1], R.sem_yb, i, y_dev(i))
-            for i in range(1, NY)
-        ]
-    )
-    arrive(ya)
-    total = R.part1[0:2, :, y_cols(0)].astype(F32)
-    for i in range(1, NY):
-        total = total + R.ya_recv[i - 1].astype(F32)
-    R.part2[...] = total.astype(BF)
-    za = go(
-        [
-            remote(R.part2.at[:, z_rows(i), :], R.za_recv.at[i - 1], R.sem_za, i, z_dev(i))
-            for i in range(1, NZ)
-        ]
-    )
-    arrive(sqy)
-    sq = R.tile_sq[1]
-    for i in range(1, NY):
-        sq = sq + R.tile_sq_y[i - 1]
-    R.tile_sq[2] = sq
-    sqz = go(
-        [
-            remote(R.tile_sq.at[2], R.tile_sq_z.at[i - 1], R.sem_sqz, i, z_dev(i))
-            for i in range(1, NZ)
+            for i in far_y
         ]
     )
 
     def ring(step):
         half = step == NY // 2
         back = step - 1
-        left = R.og_all.at[(y + NY - back) % NY, :, k, pl.ds(RA, RB)]
-        right = R.og_all.at[(y + back) % NY, :, k, pl.ds(RA, RB)]
+        left = R.og_all.at[(y + NY - back) % NY, :, k]
+        right = R.og_all.at[(y + back) % NY, :, k]
         if half:
-            left = R.og_all.at[(y + NY - back) % NY, :, k, pl.ds(RA, RB), pl.ds(0, TH)]
-            right = R.og_all.at[(y + back) % NY, :, k, pl.ds(RA, RB), pl.ds(TH, TH)]
+            left = R.og_all.at[(y + NY - back) % NY, :, k, :, pl.ds(0, TH)]
+            right = R.og_all.at[(y + back) % NY, :, k, :, pl.ds(TH, TH)]
         return go(
             [
                 remote(left, left, R.sem_ring, 2 * step, y_dev(1)),
@@ -337,22 +297,83 @@
             ]
         )
 
+    ogk = []
+
+    def to_sib(ref):
+        ogk.extend(go([remote(ref, ref, R.sem_ogk, len(ogk), sib)]))
+
+    def hand_over(step):
+        if step == NY // 2:
+            to_sib(R.og_all.at[(y + step) % NY, :, k])
+        else:
+            to_sib(R.og_all.at[(y + step) % NY, :, k])
+            to_sib(R.og_all.at[(y + NY - step) % NY, :, k])
+
     arrive(ogb1)
     hop = ring(1)
-
+    to_sib(R.og_all.at[y, :, k])
+    ld["ctx"].wait()
+    R.cs_all[x, w, pl.ds(A, S)] = mm_nt(oh_slot, R.cs_all[x, w, pl.ds(0, A)]).astype(BF)
+    cs1 = go([remote(own_cs, own_cs, R.sem_cs, 0, w_dev)])
+
+    arrive(zb)
+    total = R.part1[2, z_rows(0), :].astype(F32)
+    for i in far_z:
+        total = total + R.zb_recv[i - 1].astype(F32)
+    R.part2b[...] = total.astype(BF)
+    yb = go(
+        [
+            remote(R.part2b.at[:, y_cols(i)], R.yb_recv.at[i - 1], R.sem_yb, i, y_dev(i))
+            for i in far_y
+        ]
+    )
+    ld["wo"].wait()
+    R.wo_t[...] = R.wo_v[...].T
+    if NY // 2 >= 2:
+        arrive(hop)
+        hop = ring(2)
+        hand_over(1)
+    arrive(ya)
+    total = R.part1[0:2, :, y_cols(0)].astype(F32)
+    for i in far_y:
+        total = total + R.ya_recv[i - 1].astype(F32)
+    R.part2[...] = total.astype(BF)
+    za = go(
+        [
+            remote(R.part2.at[:, z_rows(i), :], R.za_recv.at[i - 1], R.sem_za, i, z_dev(i))
+            for i in far_z
+        ]
+    )
+    arrive(sqy)
+    sq = R.tile_sq[1]
+    for i in far_y:
+        sq = sq + R.tile_sq_y[i - 1]
+    R.tile_sq[2] = sq
+    sqz = go(
+        [
+            remote(R.tile_sq.at[2], R.tile_sq_z.at[i - 1], R.sem_sqz, i, z_dev(i))
+            for i in far_z
+        ]
+    )
+
+
+    arrive(cs1)
+    cs2 = go(
+        [remote(R.cs_all.at[x], R.cs_all.at[x], R.sem_cs, i, x_dev(i)) for i in range(1, NX)]
+    )
     arrive(sqz)
     sq = R.tile_sq[2]
-    for i in range(1, NZ):
+    for i in far_z:
         sq = sq + R.tile_sq_z[i - 1]
     inv_col = row_to_col(lax.rsqrt(sq[0:1] / D + norm_eps))
     R.inv_buf[...] = jnp.broadcast_to(inv_col, (S, HY))
     arrive(yb)
     hid_grad = R.part2b[:, y_cols(0)].astype(F32)
-    for i in range(1, NY):
+    for i in far_y:
         hid_grad = hid_grad + R.yb_recv[i - 1].astype(F32)
     arrive(za)
     total = R.part2[:, z_rows(0), :].astype(F32)
-    for i in range(1, NZ):
+    for i in far_z:
         total = total + R.za_recv[i - 1].astype(F32)
     inv_mine = R.inv_buf[z_rows(0), :]
     pre_gate = inv_mine * total[0]
@@ -377,55 +398,59 @@
     dtz = go(
         [
             remote(R.tile_dot.at[0], R.tile_dot_z.at[i - 1], R.sem_dtz, i, z_dev(i))
-            for i in range(1, NZ)
-        ]
-    )
+            for i in far_z
+        ]
+    )
+    if NY // 2 >= 3:
+        arrive(hop)
+        hop = ring(3)
+        hand_over(2)
     arrive(g1)
     g2 = to_y(R.act.at[0, :, my_cols], R.sem_g2)
     arrive(u1)
     u2 = to_z(R.act.at[1, z_rows(0), own], R.sem_u2)
     arrive(dtz)
     dt = R.tile_dot[0]
-    for i in range(1, NZ):
+    for i in far_z:
         dt = dt + R.tile_dot_z[i - 1]
     R.tile_dot[1] = dt
     dty = go(
         [
             remote(R.tile_dot.at[1], R.tile_dot_y.at[i - 1], R.sem_dty, i, y_dev(i))
-            for i in range(1, NY)
-        ]
-    )
-    arrive(oga1)
-    oga2 = to_z(R.og_all.at[:, z, k, pl.ds(0, RA)], R.sem_oga, NY)
-    steps = NY // 2
-    if steps >= 2:
+            for i in far_y
+        ]
+    )
+    if NY // 2 >= 4:
         arrive(hop)
-        hop = ring(2)
+        hop = ring(4)
+        hand_over(3)
 
     arrive(g2)
     arrive(u2)
     own_act = R.act.at[pl.ds(0, 2), :, own]
     gk = go([remote(own_act, own_act, R.sem_gk, 0, sib)])
-    arrive(h1)
-    h2 = to_y(R.act.at[2, :, my_cols], R.sem_h2)
     arrive(dty)
     dt = R.tile_dot[1]
-    for i in range(1, NY):
+    for i in far_y:
         dt = dt + R.tile_dot_y[i - 1]
     R.tile_dot[2] = dt
     dtc = go([remote(R.tile_dot.at[2], R.tile_dot_c, R.sem_dtc, 0, sib)])
     inv_col = R.inv_buf[:, 0:1]
     normed = rows_x * inv_col
+
+    def back_part(cols):
+        return mm_nt(R.act[0, :, cols], R.wg_v[:, cols]) + mm_nt(R.act[1, :, cols], R.wu_v[:, cols])
+
+    back = back_part(own)
     arrive(dtc)
     dots_col = row_to_col((R.tile_dot[2] + R.tile_dot_c[...])[0:1])
     arrive(gk)
-    slot_back = (
-        (mm_nt(R.act[0], R.wg_v[...]) + mm_nt(R.act[1], R.wu_v[...])).astype(BF).astype(F32)
-    )
+    back = back + back_part(other)
+    slot_back = back.astype(BF).astype(F32)
     delta = inv_col * (gain * slot_back - normed * (dots_col / D))
     R.delta_own[...] = delta.astype(BF)
 
-    d_cross = remote(R.delta_own, R.delta_all.at[z, k, ep], R.sem_dt, 0, cross)
+    d_cross = remote(R.delta_own, R.delta_all.at[z, k, ep], R.sem_da, 0, cross)
 
     @pl.when(off_diag)
     def _():
@@ -440,53 +465,36 @@
     ret_copies = go(
         [
             remote(R.ret_send.at[(ep + i) % NE], R.ret_recv.at[ep], R.sem_ret, i, ep_dev(i))
-            for i in range(1, NE)
-        ]
-    )
-    if steps >= 3:
-        arrive(hop)
-        hop = ring(3)
+            for i in far_e
+        ]
+    )
     slot_in = (normed * gain).astype(BF)
     store("gate_out", mm_tn(slot_in, R.act[0]).astype(BF))
-
-    @pl.when(off_diag)
-    def _():
-        d_cross.wait_recv()
-
+    arrive_whole(d_cross)
     da1 = to_y(R.delta_all.at[z, k, y, pl.ds(0, SH)], R.sem_da)
     db1 = to_z(R.delta_all.at[z, k, y, pl.ds(SH, SH)], R.sem_db)
-    arrive(h2)
-    own_hid = R.act.at[2, :, own]
-    hk = go([remote(own_hid, own_hid, R.sem_gk, 1, sib)])
-    if steps >= 4:
-        arrive(hop)
-        hop = ring(4)
+    arrive(hop)
+    hand_over(NY // 2)
     store("up_out", mm_tn(slot_in, R.act[1]).astype(BF))
     arrive(db1)
     db2 = to_y(R.delta_all.at[:, k, y, pl.ds(SH, SH)], R.sem_db, NZ)
     arrive(da1)
     da2 = to_z(R.delta_all.at[z, k, :, pl.ds(0, SH)], R.sem_da, NY)
-
-    arrive(hop)
-    arrive(oga2)
-    ogk_mine = R.og_all.at[:, :, k]
-    ogk = go([remote(ogk_mine, ogk_mine, R.sem_ogk, 0, sib)])
-    arrive(hk)
-    store("down_out", mm_tn(rows_gob, R.act[2]).astype(BF))
+    arrive(h1)
+    h2 = to_y(R.act.at[2, :, my_cols], R.sem_h2)
     arrive(ogk)
-    for g in range(NE):
-        block = R.og_all[g].reshape(BL, T)
-        R.base_send[g // 2, g % 2] = mm(R.wo_t[...], block).astype(BF)
-    bx = go(
-        [
-            remote(R.base_send.at[(x + i) % NX], R.bx_recv.at[i - 1], R.sem_bx, i, x_dev(i))
-            for i in range(1, NX)
-        ]
-    )
-    arrive(da2)
-    arrive(db2)
-    dk_mine = R.delta_all.at[:, k]
-    dk = go([remote(dk_mine, dk_mine, R.sem_dk, 0, sib)])
+
+    def base(xi):
+        for j in range(2):
+            block = R.og_all[2 * xi + j].reshape(BL, T)
+            R.base_send[xi, j] = mm(R.wo_t[...], block).astype(BF)
+
+    bx = []
+    for i in range(1, NX):
+        xi = (x + i) % NX
+        base(xi)
+        bx += go([remote(R.base_send.at[xi], R.bx_recv.at[i - 1], R.sem_bx, i, x_dev(i))])
+    base(x)
     arrive(cs2)
     for g in range(NE):
         one = mm_nt(R.og_all[g].reshape(BL, T), R.cs_all[g // 2, g % 2, pl.ds(0, A)])
@@ -494,26 +502,41 @@
             R.wo_acc[...] = one
         else:
             R.wo_acc[...] += one
-    sel = R.cs_all[:, :, pl.ds(A, S)].astype(F32).reshape(NE, NE, CAP, A)
-    for e in range(NE):
-        R.sel_perm[e] = sel[:, e].reshape(S, A).astype(BF)
-
+    arrive(da2)
+    arrive(db2)
+    dk_mine = R.delta_all.at[:, k]
+    dk = go([remote(dk_mine, dk_mine, R.sem_dk, 0, sib)])
+    arrive(h2)
+    own_hid = R.act.at[2, :, own]
+    hk = go([remote(own_hid, own_hid, R.sem_gk, 1, sib)])
+
+    def slot_part_of(kk):
+        total = None
+        for q in range(NZ):
+            block = R.delta_all[q, kk].reshape(NE * S, FS)
+            feats = pl.ds(pl.multiple_of((q * 2 + kk) * FS, 16), FS)
+            one = mm(block, R.wo_v[feats, :])
+            total = one if total is None else total + one
+        return total
+
+    slots = slot_part_of(k)
     arrive(dk)
-    slots = None
-    for q in range(NZ * 2):
-        block = R.delta_all[q // 2, q % 2].reshape(NE * S, FS)
-        one = mm(block, R.wo_v[pl.ds(q * FS, FS), :])
-        slots = one if slots is None else slots + one
+    slots = slots + slot_part_of(1 - k)
     slots = slots.reshape(NE, NE, CAP, A)
     for g in range(NE):
         R.msg_send[g] = slots[:, g].reshape(S, A).astype(BF)
     msg_copies = go(
         [
             remote(R.msg_send.at[(ep + i) % NE], R.msg_recv.at[ep], R.sem_msg, i, ep_dev(i))
-            for i in range(1, NE)
+            for i in far_e
         ]
     )
     R.msg_recv[ep] = R.msg_send[ep]
+    arrive(hk)
+    store("down_out", mm_tn(rows_gob, R.act[2]).astype(BF))
+    sel = R.cs_all[:, :, pl.ds(A, S)].astype(F32).reshape(NE, NE, CAP, A)
+    for e in range(NE):
+        R.sel_perm[e] = sel[:, e].reshape(S, A).astype(BF)
     arrive(bx)
     total = R.base_send[x].astype(F32)
     for i in range(1, NX):
@@ -533,7 +556,7 @@
 
     arrive(msg_copies)
     picked = R.msg_recv[0].astype(F32)
-    for i in range(1, NE):
+    for i in far_e:
         picked = picked + R.msg_recv[i].astype(F32)
     slot_part = mm_tn(picked.astype(BF), oh_slot)
     arrive(bw)
@@ -684,11 +707,10 @@
         sem_in=dma((11,)),
         sem_out=dma((6,)),
         sem_a=dma((2, NE)),
-        sem_ogt=dma((2, 1)),
-        sem_oga=dma((2, NY + NZ)),
+        sem_oga=dma((2, 1)),
         sem_ogb=dma((2, NZ)),
         sem_ring=dma((2, NY + 2)),
-        sem_ogk=dma((2, 1)),
+        sem_ogk=dma((2, NY + 2)),
         sem_cs=dma((2, max(NX, 1))),
         sem_core=dma((2, 1)),
         sem_ya=dma((2, NY)),
@@ -709,7 +731,6 @@
         sem_h2=dma((2, NY)),
         sem_gk=dma((2, 2)),
         sem_ret=dma((2, NE)),
-        sem_dt=dma((2, 1)),
         sem_da=dma((2, NY + NZ)),
         sem_db=dma((2, NY + NZ)),
         sem_dk=dma((2, 1)),

time: 99.5 us -> 94 us (0.945)
  the two profiles are of different devices: /device:TPU:72 before, /device:TPU:1 now
where the time goes in v4:
time: 94 us; the launch traced here: 92.2 us
  Pallas kernels  91.5 us (97%)
    pallas_call x1, Pallas kernels, shards(): pl.pallas_call(functools.partial(kernel, dims, spec), out_shape=out_shape...  89.1 us
    pallas_call x1, Pallas kernels, shards(): pl.pallas_call(copy_out, out_shape=out_shape, in_specs=[hbm] * len(outs),...  2.44 us

profile of v4, /device:TPU:1, one launch (start us, length us, event | category | flops | bytes accessed | tf_op | source)
XLA Modules:
  0.0 92.2 jit_solution(4934096254554367705)
XLA Ops:
  0.6 89.1 %shard_map.154 = (bf16[112,256]{1,0:T(8,128)(2,1)}, bf16[256,256]{1,0:T(8,128)(2,1)}, bf16[896,256]{1,0:T(8,128)(2,1)}, bf16[112,2048]{1,0:T(8,128)(2,1)}, bf16[...) custom-call(s32[8,8]{1,0:T(8,128)} %bitcast.20, s32[1,8]{1,0:T(1,128)} %refs_1_.1, f32[8,8]{1,0:T(8,128)} %bitcast.21, ...), custom_call_target="tpu_custom_call" | custom-call | tf_op jit(solution)/shard_map/pallas_call | solution.py:742
  89.7 2.4 %shard_map.155 = (bf16[112,256]{1,0:T(8,128)(2,1)}, bf16[256,256]{1,0:T(8,128)(2,1)}, bf16[896,256]{1,0:T(8,128)(2,1)}, bf16[112,2048]{1,0:T(8,128)(2,1)}, bf16[...) custom-call(bf16[112,256]{1,0:T(8,128)(2,1)} %get-tuple-element.18.refs_0_, bf16[256,256]{1,0:T(8,128)(2,1)} %get-tuple-element.19.refs_1_, ...), custom_call_target="tpu_custom_call" | custom-call | tf_op jit(solution)/shard_map/pallas_call | solution.py:752

commit v5 on v4

--- a/solution.py
+++ b/solution.py
@@ -312,9 +312,6 @@
     arrive(ogb1)
     hop = ring(1)
     to_sib(R.og_all.at[y, :, k])
-    ld["ctx"].wait()
-    R.cs_all[x, w, pl.ds(A, S)] = mm_nt(oh_slot, R.cs_all[x, w, pl.ds(0, A)]).astype(BF)
-    cs1 = go([remote(own_cs, own_cs, R.sem_cs, 0, w_dev)])
 
     arrive(zb)
     total = R.part1[2, z_rows(0), :].astype(F32)
@@ -357,10 +354,9 @@
     )
 
 
-    arrive(cs1)
-    cs2 = go(
-        [remote(R.cs_all.at[x], R.cs_all.at[x], R.sem_cs, i, x_dev(i)) for i in range(1, NX)]
-    )
+    ld["ctx"].wait()
+    R.cs_all[x, w, pl.ds(A, S)] = mm_nt(oh_slot, R.cs_all[x, w, pl.ds(0, A)]).astype(BF)
+    cs1 = go([remote(own_cs, own_cs, R.sem_cs, 0, w_dev)])
     arrive(sqz)
     sq = R.tile_sq[2]
     for i in far_z:
@@ -425,6 +421,10 @@
         hop = ring(4)
         hand_over(3)
 
+    arrive(cs1)
+    cs2 = go(
+        [remote(R.cs_all.at[x], R.cs_all.at[x], R.sem_cs, i, x_dev(i)) for i in range(1, NX)]
+    )
     arrive(g2)
     arrive(u2)
     own_act = R.act.at[pl.ds(0, 2), :, own]
@@ -475,13 +475,10 @@
     db1 = to_z(R.delta_all.at[z, k, y, pl.ds(SH, SH)], R.sem_db)
     arrive(hop)
     hand_over(NY // 2)
-    store("up_out", mm_tn(slot_in, R.act[1]).astype(BF))
     arrive(db1)
     db2 = to_y(R.delta_all.at[:, k, y, pl.ds(SH, SH)], R.sem_db, NZ)
     arrive(da1)
     da2 = to_z(R.delta_all.at[z, k, :, pl.ds(0, SH)], R.sem_da, NY)
-    arrive(h1)
-    h2 = to_y(R.act.at[2, :, my_cols], R.sem_h2)
     arrive(ogk)
 
     def base(xi):
@@ -494,7 +491,10 @@
         xi = (x + i) % NX
         base(xi)
         bx += go([remote(R.base_send.at[xi], R.bx_recv.at[i - 1], R.sem_bx, i, x_dev(i))])
+    arrive(h1)
+    h2 = to_y(R.act.at[2, :, my_cols], R.sem_h2)
     base(x)
+    store("up_out", mm_tn(slot_in, R.act[1]).astype(BF))
     arrive(cs2)
     for g in range(NE):
         one = mm_nt(R.og_all[g].reshape(BL, T), R.cs_all[g // 2, g % 2, pl.ds(0, A)])

time: 94 us -> 94 us (level)
  no operation moved by 1% of the time
where the time goes in v5:
time: 94 us; the launch traced here: 92.2 us
  Pallas kernels  91.6 us (97%)
    pallas_call x1, Pallas kernels, shards(): pl.pallas_call(functools.partial(kernel, dims, spec), out_shape=out_shape...  89.1 us
    pallas_call x1, Pallas kernels, shards(): pl.pallas_call(copy_out, out_shape=out_shape, in_specs=[hbm] * len(outs),...  2.44 us

profile of v5, /device:TPU:1, one launch (start us, length us, event | category | flops | bytes accessed | tf_op | source)
XLA Modules:
  0.0 92.2 jit_solution(4845646687050541288)
XLA Ops:
  0.6 89.1 %shard_map.154 = (bf16[112,256]{1,0:T(8,128)(2,1)}, bf16[256,256]{1,0:T(8,128)(2,1)}, bf16[896,256]{1,0:T(8,128)(2,1)}, bf16[112,2048]{1,0:T(8,128)(2,1)}, bf16[...) custom-call(s32[8,8]{1,0:T(8,128)} %bitcast.20, s32[1,8]{1,0:T(1,128)} %refs_1_.1, f32[8,8]{1,0:T(8,128)} %bitcast.21, ...), custom_call_target="tpu_custom_call" | custom-call | tf_op jit(solution)/shard_map/pallas_call | solution.py:742
  89.8 2.4 %shard_map.155 = (bf16[112,256]{1,0:T(8,128)(2,1)}, bf16[256,256]{1,0:T(8,128)(2,1)}, bf16[896,256]{1,0:T(8,128)(2,1)}, bf16[112,2048]{1,0:T(8,128)(2,1)}, bf16[...) custom-call(bf16[112,256]{1,0:T(8,128)(2,1)} %get-tuple-element.18.refs_0_, bf16[256,256]{1,0:T(8,128)(2,1)} %get-tuple-element.19.refs_1_, ...), custom_call_target="tpu_custom_call" | custom-call | tf_op jit(solution)/shard_map/pallas_call | solution.py:752
